TPU v7x, 128 devices: a whole 4x4x4 slice. The times are simulated.
128 devices in a mesh: vec: 8 (over y, z_lo), gz: 16 (over x, z_hi, core).
Axes of the slice: x: 4, y: 4, z: 4 (z_hi: 2, z_lo: 2; z = z_hi * 2 + z_lo), core: 2. Of those that a mesh axis runs over, the one named last changes fastest.
Arguments:
- vectors: bfloat16 [1024, 3, 2, 8192], P('vec', None, None, 'gz'), may hold values from -6 to 6
- links: float32 [3, 3, 3, 2, 8192], P(None, None, None, None, 'gz'), may hold values from -4 to 4
- dirs: int32 [6], replicated, may hold values from 0 to 5, each once
- moms: int32 [2, 3], replicated, may hold values from -2 to 2
Outputs:
- elementals: float32 [6, 2, 2, 1024, 1024], P(None, None, None, ('vec', 'gz'))
Inputs may be any that keep to these rules, and one draw needn't show every extreme that they name: `dirs`: each of the six directions appears exactly once.
All inputs are finite; a program needn't handle non-finite values.
Results may differ from a plain program's by a relative error of at most 0.0039.
Values may be sent and summed in bfloat16 or wider, within the bound.
A program may use at most 192 MiB of HBM per device.

v0:
```python
import math

import jax
import jax.numpy as jnp
from jax import lax
from jax.sharding import PartitionSpec as P

LX = 32
LY = 8


def from_behind(shard, axis, by):
    peers = lax.axis_size(axis)
    return lax.ppermute(shard, axis, [(i, (i + by) % peers) for i in range(peers)])


def extended_2(cells, sides, width):
    for axis, dim in sides:
        count = lax.axis_size(axis)
        head = lax.slice_in_dim(cells, 0, width, axis=dim)
        tail = lax.slice_in_dim(cells, cells.shape[dim] - width, cells.shape[dim], axis=dim)
        cells = jnp.concatenate(
            [
                lax.ppermute(tail, axis, [(i, (i + 1) % count) for i in range(count)]),
                cells,
                lax.ppermute(head, axis, [((i + 1) % count, i) for i in range(count)]),
            ],
            axis=dim,
        )
    return cells


def split_up(shard, dim, peers):
    before, after = (shard.shape[:dim], shard.shape[dim + 1 :])
    return jnp.moveaxis(shard.reshape(*before, peers, -1, *after), dim, 0)


def sum_at_owner(shard, axis, dim):
    blocks = split_up(shard, dim, lax.axis_size(axis))
    arrived = lax.all_to_all(blocks, axis, split_axis=0, concat_axis=0, tiled=True)
    return arrived.sum(axis=0)


def colour_apply(link_real, link_imag, vec_real, vec_imag):
    out_real = jnp.float32(0.0)
    out_imag = jnp.float32(0.0)
    for column in range(3):
        left_real = link_real[None, :, column]
        left_imag = link_imag[None, :, column]
        right_real = vec_real[:, None, column].astype(jnp.float32)
        right_imag = vec_imag[:, None, column].astype(jnp.float32)
        out_real = out_real + left_real * right_real - left_imag * right_imag
        out_imag = out_imag + left_real * right_imag + left_imag * right_real
    return (out_real, out_imag)


def neighbour(field, stride, extent, position, forward):
    if forward:
        inside = jnp.roll(field, -stride, axis=-1)
        beside_all = jnp.roll(field, (extent - 1) * stride, axis=-1)
        return jnp.where(position == extent - 1, beside_all, inside)
    inside = jnp.roll(field, stride, axis=-1)
    beside_all = jnp.roll(field, -(extent - 1) * stride, axis=-1)
    return jnp.where(position == 0, beside_all, inside)


def displace(extended, links, lower_links, direction, plane, x_index, y_index):
    sites = links.shape[-1]
    axis_index = direction % 3
    link = links[axis_index]
    if direction < 3:
        if axis_index == 0:
            moved = neighbour(extended[..., plane : plane + sites], 1, LX, x_index, True)
        elif axis_index == 1:
            moved = neighbour(extended[..., plane : plane + sites], LX, LY, y_index, True)
        else:
            moved = extended[..., 2 * plane : 2 * plane + sites]
        link_real = link[:, :, 0]
        link_imag = link[:, :, 1]
    else:
        if axis_index == 0:
            moved = neighbour(extended[..., plane : plane + sites], 1, LX, x_index, False)
            behind = neighbour(link, 1, LX, x_index, False)
        elif axis_index == 1:
            moved = neighbour(extended[..., plane : plane + sites], LX, LY, y_index, False)
            behind = neighbour(link, LX, LY, y_index, False)
        else:
            moved = extended[..., 0:sites]
            behind = jnp.concatenate((lower_links, link), axis=-1)[..., 0:sites]
        link_real = jnp.swapaxes(behind[:, :, 0], 0, 1)
        link_imag = -jnp.swapaxes(behind[:, :, 1], 0, 1)
    disp_real, disp_imag = colour_apply(link_real, link_imag, moved[:, :, 0], moved[:, :, 1])
    return jnp.stack((disp_real.astype(jnp.bfloat16), disp_imag.astype(jnp.bfloat16)), axis=2)


def on_device(vectors, links, dirs, moms):
    sites = vectors.shape[-1]
    plane = LY * LX
    depth = sites // plane
    shards = lax.axis_size("gz")
    flat = jnp.arange(sites, dtype=jnp.int32)
    x_index = flat % LX
    y_index = flat // LX % LY
    z_index = lax.axis_index("gz") * depth + flat // plane
    lower_links = from_behind(links[2, :, :, :, sites - plane :], "gz", 1)
    gathered = lax.all_gather(vectors, "vec", axis=0, tiled=True)
    extended = extended_2(gathered, (("gz", 3),), plane)
    momenta = moms.astype(jnp.float32)
    theta = (
        momenta[:, 0, None] * x_index.astype(jnp.float32) / LX
        + momenta[:, 1, None] * y_index.astype(jnp.float32) / LY
        + momenta[:, 2, None] * z_index.astype(jnp.float32) / (depth * shards)
    ) * (2.0 * math.pi)
    cosine = jnp.cos(theta)[:, None, None]
    sine = jnp.sin(theta)[:, None, None]
    own_f = vectors.astype(jnp.float32)
    real_part = own_f[:, :, 0][None]
    imag_part = own_f[:, :, 1][None]
    phased_real = (cosine * real_part - sine * imag_part).astype(jnp.bfloat16)
    phased_imag = (sine * real_part + cosine * imag_part).astype(jnp.bfloat16)
    left_side = jnp.stack(
        (
            jnp.stack((phased_real, phased_imag), axis=3),
            jnp.stack((-phased_imag, phased_real), axis=3),
        ),
        axis=0,
    )
    terms = []
    for direction in range(6):
        displaced = displace(extended, links, lower_links, direction, plane, x_index, y_index)
        product = jnp.einsum(
            "qpicrs,jcrs->pqij", left_side, displaced, preferred_element_type=jnp.float32
        )
        terms.append(sum_at_owner(product, "gz", 2))
    stacked = jnp.stack(terms, axis=0)
    select = (dirs[:, None] == jnp.arange(6, dtype=jnp.int32)[None, :]).astype(jnp.float32)
    chosen = jnp.einsum("dk,kpqij->dpqij", select, stacked, precision=lax.Precision.HIGHEST)
    return chosen * (1.0 / math.sqrt(3.0 * sites * shards))


def solution(mesh):
    placed = (P("vec", None, None, "gz"), P(None, None, None, None, "gz"), P(), P())
    return jax.shard_map(
        on_device,
        mesh=mesh,
        in_specs=placed,
        out_specs=P(None, None, None, ("vec", "gz"), None),
        check_vma=False,
    )
```

profile of v0, /device:TPU:0, one launch (start us, length us, event | category | flops | bytes accessed | tf_op | source)
XLA Modules:
  0.0 507.1 jit_solution(9093775337054759167)
XLA Ops:
  6.5 2.3 copy_convert_fusion
  9.6 0.8 slice_bitcast_fusion.50
  12.6 1.9 maximum_bitcast_fusion.24
  21.8 118.8 %all-gather.2.cloned.1.call-done = bf16[1024,3,2,512]{3,0,2,1:T(8,128)(2,1)} async-done(((bf16[128,3,2,512]{3,0,2,1:T(8,128)(2,1)}), bf16[1024,3,2,512]{3,0,2,1:T(8,128)(2,1)}) %all-gather.2.cloned.1.call-update) | async-done | bytes 6291472 | tf_op jit(solution)/shard_map/all_gather | solution.py:106
  140.6 7.9 %fusion.92 = (bf16[1024,3,2,481]{3,0,2,1:T(8,128)(2,1)S(1)}, bf16[1024,3,2,481]{3,0,2,1:T(8,128)(2,1)S(1)}) fusion(bf16[1024,3,2,512]{3,0,2,1:T(8,128)(2,1)} %all-gather.2.cloned.1.call-done), kind=kLoop, calls=%fused_computation.256 | loop fusion | bytes 23642112 | tf_op jit(solution)/shard_map/jit(_roll_static)/slice | solution.py:63
  148.5 1.9 fusion.93
  150.3 2.5 fusion.90
  152.8 5.0 fusion.91
  157.8 17.8 %maximum_select_fusion = (bf16[1024,3,2,512]{3,0,2,1:T(8,128)(2,1)}, bf16[1024,3,2,512]{3,0,2,1:T(8,128)(2,1)}) fusion(bf16[1024,3,2,481]{3,0,2,1:T(8,128)(2,1)S(1)} %get-tuple-element.49, bf16[1024,3,2,31]{3,0,2,1:T(8,128)(2,1)} %get-tuple-element.51, bf16[1024,3,2,1]{3,0,2,1:T(8,128)(2,1)} %get-tuple-element.45, ...), kind=kLoop, calls=%fused_computation | loop fusion | flops 56623104 | bytes 37749760 | tf_op jit(solution)/shard_map/jit(_where)/select_n | solution.py:61
  175.6 3.3 slice_bitcast_fusion.11
  178.9 0.9 fusion.58
  180.4 4.9 subtract_convert_fusion.5
  185.4 3.4 fusion.23
  188.8 1.4 copy.130
  190.3 7.1 %all-to-all-start = ((f32[16,2,2,8,1024]{4,3,1,2,0:T(8,128)}), f32[16,2,2,8,1024]{4,3,1,2,0:T(8,128)}, u32[]{:S(2)}, u32[]{:S(2)}) async-start(f32[16,2,2,8,1024]{4,3,1,2,0:T(8,128)} %bitcast.488), calls=%async_computation | async-start | bytes 4194304 | tf_op jit(solution)/shard_map/all_to_all | solution.py:40
  197.4 10.2 %fusion.88 = (bf16[1024,3,2,288]{3,0,2,1:T(8,128)(2,1)}, bf16[1024,3,2,288]{3,0,2,1:T(8,128)(2,1)}) fusion(bf16[1024,3,2,512]{3,0,2,1:T(8,128)(2,1)} %all-gather.2.cloned.1.call-done), kind=kLoop, calls=%fused_computation.252 | loop fusion | bytes 14155776 | tf_op jit(solution)/shard_map/jit(_roll_static)/slice | solution.py:63
  207.6 4.4 fusion.89
  212.1 1.9 fusion.86
  213.9 6.4 %fusion.87 = (bf16[1024,3,2,480]{3,0,2,1:T(8,128)(2,1)}, bf16[1024,3,2,480]{3,0,2,1:T(8,128)(2,1)}) fusion(bf16[1024,3,2,512]{3,0,2,1:T(8,128)(2,1)S(1)} %bitcast.481), kind=kLoop, calls=%fused_computation.251 | loop fusion | bytes 23592960 | tf_op jit(solution)/shard_map/jit(_roll_static)/slice | solution.py:62
  220.4 17.1 %maximum_select_fusion.1 = (bf16[1024,3,2,512]{3,0,2,1:T(8,128)(2,1)}, bf16[1024,3,2,512]{3,0,2,1:T(8,128)(2,1)S(1)}) fusion(bf16[1024,3,2,288]{3,0,2,1:T(8,128)(2,1)} %get-tuple-element.39, bf16[1024,3,2,224]{3,0,2,1:T(8,128)(2,1)} %get-tuple-element.41, bf16[1024,3,2,32]{3,0,2,1:T(8,128)(2,1)} %get-tuple-element.35, ...), kind=kLoop, calls=%fused_computation.5 | loop fusion | flops 56623104 | bytes 37749760 | tf_op jit(solution)/shard_map/jit(_where)/select_n | solution.py:61
  237.5 3.3 slice_bitcast_fusion.9
  241.9 5.3 %subtract_convert_fusion.4 = (bf16[1024,3,1,512]{3,0,2,1:T(8,128)(2,1)S(1)}, bf16[1024,3,1,512]{3,0,2,1:T(8,128)(2,1)S(1)}) fusion(f32[1024,512]{1,0:T(8,128)S(1)} %get-tuple-element.84, f32[3,512]{1,0:T(4,128)S(1)} %bitcast.513, f32[1024,512]{1,0:T(8,128)S(1)} %get-tuple-element.81, f32[3,512]{1,0:T(4,128)S(1)} %bitcast.514, ...), kind=kLoop, calls=%fused_computation.37 | loop fusion | flops 37748736 | bytes 18911232 | tf_op jit(solution)/shard_map/convert_element_type | solution.py:93
  247.2 4.8 fusion.22
  252.1 1.6 copy.129
  253.7 3.2 fusion.85
  257.4 4.9 collective-permute-start
  263.3 2.0 fusion.41
  265.3 2.0 slice_bitcast_fusion.3
  267.4 4.9 subtract_convert_fusion.2
  272.4 3.4 fusion.20
  275.8 1.5 copy.127
  277.3 5.4 %all-to-all-start.1 = ((f32[16,2,2,8,1024]{4,3,1,2,0:T(8,128)}), f32[16,2,2,8,1024]{4,3,1,2,0:T(8,128)}, u32[]{:S(2)}, u32[]{:S(2)}) async-start(f32[16,2,2,8,1024]{4,3,1,2,0:T(8,128)} %bitcast.489), calls=%async_computation.1 | async-start | bytes 4194304 | tf_op jit(solution)/shard_map/all_to_all | solution.py:40
  282.7 2.7 fusion.34
  285.6 0.9 fusion.35
  286.5 6.3 %subtract_convert_fusion.1 = (bf16[1024,3,1,512]{3,0,2,1:T(8,128)(2,1)}, bf16[1024,3,1,512]{3,0,2,1:T(8,128)(2,1)}) fusion(f32[1024,512]{1,0:T(8,128)S(1)} %get-tuple-element.66, f32[3,512]{1,0:T(4,128)S(1)} %copy-done.18, f32[1024,512]{1,0:T(8,128)S(1)} %get-tuple-element.63, f32[3,512]{1,0:T(4,128)S(1)} %copy-done.27, ...), kind=kLoop, calls=%fused_computation.31 | loop fusion | flops 37748736 | bytes 18911232 | tf_op jit(solution)/shard_map/convert_element_type | solution.py:93
  292.8 59.5 %all-to-all-done.1 = f32[16,2,2,8,1024]{4,3,1,2,0:T(8,128)} async-done(((f32[16,2,2,8,1024]{4,3,1,2,0:T(8,128)}), f32[16,2,2,8,1024]{4,3,1,2,0:T(8,128)}, u32[]{:S(2)}, u32[]{:S(2)}) %all-to-all-start.1) | async-done | bytes 2097184 | tf_op jit(solution)/shard_map/all_to_all | solution.py:40
  352.3 6.1 %all-to-all-start.3 = ((f32[16,2,2,8,1024]{4,3,1,2,0:T(8,128)}), f32[16,2,2,8,1024]{4,3,1,2,0:T(8,128)}, u32[]{:S(2)}, u32[]{:S(2)}) async-start(f32[16,2,2,8,1024]{4,3,1,2,0:T(8,128)} %bitcast.450), calls=%async_computation.3 | async-start | bytes 4194304 | tf_op jit(solution)/shard_map/all_to_all | solution.py:40
  358.4 7.3 %fusion.19 = f32[2,2,16,8,1024]{4,3,2,0,1:T(8,128)S(1)} fusion(bf16[1024,3,1,512]{3,0,2,1:T(8,128)(2,1)} %get-tuple-element.15, bf16[1024,3,1,512]{3,0,2,1:T(8,128)(2,1)} %get-tuple-element.14, bf16[1,2,128,3,2,512]{5,2,4,3,1,0:T(8,128)(2,1)} %get-tuple-element.95, bf16[1,2,128,3,2,512]{5,2,4,3,1,0:T(8,128)(2,1)} %get-tuple-element.94), kind=kOutput, calls=%fused_computation.60 | convolution fusion | flops 3240099840 | bytes 11534336 | tf_op jit(solution)/shard_map/qpicrs,jcrs->pqij/dot_general | solution.py:131
  365.7 1.4 copy.126
  367.2 3.9 constant_dynamic-update-slice_fusion.3
  371.1 6.1 %constant_dynamic-update-slice_fusion.2 = (bf16[1024,3,2,768]{3,0,2,1:T(8,128)(2,1)}, bf16[1024,3,2,768]{3,0,2,1:T(8,128)(2,1)}) fusion(bf16[1024,3,2,768]{3,0,2,1:T(8,128)(2,1)} %constant_dynamic-update-slice_fusion.3, bf16[1024,3,2,512]{3,0,2,1:T(8,128)(2,1)S(1)} %bitcast.483), kind=kLoop, calls=%fused_computation.169 | loop fusion | bytes 18874368 | tf_op jit(solution)/shard_map/concatenate | solution.py:22
  377.2 3.9 constant_dynamic-update-slice_fusion
  381.1 3.7 slice_bitcast_fusion.7
  384.8 5.1 fusion.46
  389.9 7.4 %all-to-all-start.4 = ((f32[16,2,2,8,1024]{4,3,1,2,0:T(8,128)}), f32[16,2,2,8,1024]{4,3,1,2,0:T(8,128)S(1)}, u32[]{:S(2)}, u32[]{:S(2)}) async-start(f32[16,2,2,8,1024]{4,3,1,2,0:T(8,128)} %bitcast.490), calls=%async_computation.4 | async-start | bytes 4194304 | tf_op jit(solution)/shard_map/all_to_all | solution.py:40
  397.4 8.4 %subtract_convert_fusion.3 = (bf16[1024,3,1,512]{3,0,2,1:T(8,128)(2,1)S(1)}, bf16[1024,3,1,512]{3,0,2,1:T(8,128)(2,1)S(1)}) fusion(f32[1024,512]{1,0:T(8,128)} %get-tuple-element.78, f32[3,512]{1,0:T(4,128)S(1)} %bitcast.507, f32[1024,512]{1,0:T(8,128)} %get-tuple-element.160, f32[3,512]{1,0:T(4,128)S(1)} %bitcast.508, f32[1024,512]{1,0:T(8,128)} %get-tuple-element.79, ...), kind=kLoop, calls=%fused_computation.35 | loop fusion | flops 37748736 | bytes 18911232 | tf_op jit(solution)/shard_map/convert_element_type | solution.py:93
  405.9 3.4 fusion.21
  409.3 1.4 copy.128
  411.4 5.1 %fusion.28 = (f32[1024,512]{1,0:T(8,128)}, f32[1024,512]{1,0:T(8,128)}, f32[1024,512]{1,0:T(8,128)}, f32[1024,512]{1,0:T(8,128)}, f32[1024,512]{1,0:T(8,128)}, /*index=5*/f32[1024,512]{1,0:T(8,128)}) fusion(bf16[1024,3,512]{2,0,1:T(8,128)(2,1)S(1)} %get-tuple-element.25, bf16[1024,3,512]{2,0,1:T(8,128)(2,1)S(1)} %get-tuple-element.24), kind=kLoop, calls=%fused_computation.79 | loop fusion | flops 3145728 | bytes 18874368 | tf_op jit(solution)/shard_map/mul | solution.py:52
  416.4 10.0 %all-to-all-done.4 = f32[16,2,2,8,1024]{4,3,1,2,0:T(8,128)S(1)} async-done(((f32[16,2,2,8,1024]{4,3,1,2,0:T(8,128)}), f32[16,2,2,8,1024]{4,3,1,2,0:T(8,128)S(1)}, u32[]{:S(2)}, u32[]{:S(2)}) %all-to-all-start.4) | async-done | bytes 2097184 | tf_op jit(solution)/shard_map/all_to_all | solution.py:40
  426.5 5.0 all-to-all-start.2
  431.5 7.8 %subtract_convert_fusion = (bf16[1024,3,1,512]{3,0,2,1:T(8,128)(2,1)S(1)}, bf16[1024,3,1,512]{3,0,2,1:T(8,128)(2,1)S(1)}) fusion(f32[1024,512]{1,0:T(8,128)} %get-tuple-element.60, f32[3,512]{1,0:T(4,128)S(1)} %copy-done.21, f32[1024,512]{1,0:T(8,128)} %get-tuple-element.167, f32[3,512]{1,0:T(4,128)S(1)} %copy-done.24, f32[1024,512]{1,0:T(8,128)} %get-tuple-element.61, ...), kind=kLoop, calls=%fused_computation.29 | loop fusion | flops 37748736 | bytes 18911232 | tf_op jit(solution)/shard_map/convert_element_type | solution.py:93
  439.4 3.4 fusion.18
  442.8 1.5 copy.125
  444.3 16.4 %all-to-all-done.2 = f32[16,2,2,8,1024]{4,3,1,2,0:T(8,128)} async-done(((f32[16,2,2,8,1024]{4,3,1,2,0:T(8,128)}), f32[16,2,2,8,1024]{4,3,1,2,0:T(8,128)}, u32[]{:S(2)}, u32[]{:S(2)}) %all-to-all-start.2) | async-done | bytes 2097184 | tf_op jit(solution)/shard_map/all_to_all | solution.py:40
  460.7 5.0 all-to-all-start.5
  465.7 1.7 reduce_sum.54
  467.5 1.7 reduce_sum.55
  469.4 1.7 reduce_sum.57
  471.5 1.7 reduce_sum.56
  473.4 21.5 %all-to-all-done.5 = f32[16,2,2,8,1024]{4,3,1,2,0:T(8,128)} async-done(((f32[16,2,2,8,1024]{4,3,1,2,0:T(8,128)}), f32[16,2,2,8,1024]{4,3,1,2,0:T(8,128)}, u32[]{:S(2)}, u32[]{:S(2)}) %all-to-all-start.5) | async-done | bytes 2097184 | tf_op jit(solution)/shard_map/all_to_all | solution.py:40
  494.9 1.7 reduce_sum.59
  496.8 1.3 stack.87
  498.7 1.3 copy.31
  (170 shorter events, 15.6 us)
Async XLA Ops:
  6.5 134.0 %all-gather.2.cloned.1.call-start = ((), (), s32[]{:S(2)}) async-start(), calls=%async_computation.6 | async-start | bytes 7077888 | tf_op jit(solution)/shard_map/all_gather | solution.py:106
  9.6 7.1 %collective-permute-start.1 = (f32[3,3,2,256]{3,2,1,0:T(2,128)S(1)}, f32[3,3,2,256]{3,2,1,0:T(2,128)S(1)}, u32[]{:S(2)}, u32[]{:S(2)}) collective-permute-start(f32[3,3,2,256]{3,2,1,0:T(2,128)S(1)} %slice_bitcast_fusion.53), channel_id=1, source_target_pairs={{0,1},{1,2},{2,3},{3,4},{4,5},{5,6},{6,7},{7,8},{8,9},{9,10},{10,1... | collective-permute-start | bytes 55304 | tf_op jit(solution)/shard_map/ppermute | solution.py:14
  140.6 7.9 %copy-start = (bf16[1024,3,2,512]{3,0,2,1:T(8,128)(2,1)S(1)}, bf16[1024,3,2,512]{3,0,2,1:T(8,128)(2,1)}, u32[]{:S(2)}) copy-start(bf16[1024,3,2,512]{3,0,2,1:T(8,128)(2,1)} %all-gather.2.cloned.1.call-done) | copy-start | bytes 18874372
  180.4 5.0 copy-start.2
  180.4 5.0 copy-start.7
  190.3 17.3 %slice-start = ((s8[6291456]{0:T(1024)(128)(4,1)}), s8[2097152]{0:T(1024)(128)(4,1)S(1)}, s32[]{:S(2)}) async-start(s8[6291456]{0:T(1024)(128)(4,1)} %bitcast.480), calls=%async_computation.7 | async-start | bytes 4194304
  190.3 87.0 %all-to-all-start = ((f32[16,2,2,8,1024]{4,3,1,2,0:T(8,128)}), f32[16,2,2,8,1024]{4,3,1,2,0:T(8,128)}, u32[]{:S(2)}, u32[]{:S(2)}) async-start(f32[16,2,2,8,1024]{4,3,1,2,0:T(8,128)} %bitcast.488), calls=%async_computation | async-start | bytes 4194304 | tf_op jit(solution)/shard_map/all_to_all | solution.py:40
  197.4 10.3 %slice-start.1 = ((s8[6291456]{0:T(1024)(128)(4,1)}), s8[4194304]{0:T(1024)(128)(4,1)S(1)}, s32[]{:S(2)}) async-start(s8[6291456]{0:T(1024)(128)(4,1)} %bitcast.480), calls=%async_computation.8 | async-start | bytes 8388608
  241.9 5.4 %copy-start.3 = (bf16[1,2,128,3,2,512]{5,2,4,3,1,0:T(8,128)(2,1)S(1)}, bf16[1,2,128,3,2,512]{5,2,4,3,1,0:T(8,128)(2,1)}, u32[]{:S(2)}) copy-start(bf16[1,2,128,3,2,512]{5,2,4,3,1,0:T(8,128)(2,1)} %get-tuple-element.94) | copy-start | bytes 4718596
  252.1 10.2 %slice-start.4 = ((s8[6291456]{0:T(1024)(128)(4,1)}), s8[4194304]{0:T(1024)(128)(4,1)S(1)}, s32[]{:S(2)}) async-start(s8[6291456]{0:T(1024)(128)(4,1)} %bitcast.484), calls=%async_computation.11 | async-start | bytes 8388608
  253.7 8.6 %slice-start.5 = ((s8[6291456]{0:T(1024)(128)(4,1)}), s8[2097152]{0:T(1024)(128)(4,1)S(1)}, s32[]{:S(2)}) async-start(s8[6291456]{0:T(1024)(128)(4,1)} %bitcast.484), calls=%async_computation.12 | async-start | bytes 4194304
  256.9 110.3 %collective-permute-start.2 = (bf16[1024,3,2,256]{3,0,2,1:T(8,128)(2,1)}, bf16[1024,3,2,256]{3,0,2,1:T(8,128)(2,1)}, u32[]{:S(2)}, u32[]{:S(2)}) collective-permute-start(bf16[1024,3,2,256]{3,0,2,1:T(8,128)(2,1)} %get-tuple-element.30), channel_id=1, source_target_pairs={{0,1},{1,2},{2,3},{3,4},{4,5},{5,6},{6,7},{7,8},{8,9},{9,10},{10,1... | collective-permute-start | bytes 9437192 | tf_op jit(solution)/shard_map/ppermute | solution.py:24
  257.4 119.8 %collective-permute-start = (bf16[1024,3,2,256]{3,0,2,1:T(8,128)(2,1)}, bf16[1024,3,2,256]{3,0,2,1:T(8,128)(2,1)}, u32[]{:S(2)}, u32[]{:S(2)}) collective-permute-start(bf16[1024,3,2,256]{3,0,2,1:T(8,128)(2,1)} %get-tuple-element.31), channel_id=1, source_target_pairs={{1,0},{2,1},{3,2},{4,3},{5,4},{6,5},{7,6},{8,7},{9,8},{10,9},{11,1... | collective-permute-start | bytes 9437192 | tf_op jit(solution)/shard_map/ppermute | solution.py:26
  265.3 2.1 copy-start.1
  267.4 4.9 copy-start.4
  267.4 4.9 copy-start.8
  277.3 75.0 %all-to-all-start.1 = ((f32[16,2,2,8,1024]{4,3,1,2,0:T(8,128)}), f32[16,2,2,8,1024]{4,3,1,2,0:T(8,128)}, u32[]{:S(2)}, u32[]{:S(2)}) async-start(f32[16,2,2,8,1024]{4,3,1,2,0:T(8,128)} %bitcast.489), calls=%async_computation.1 | async-start | bytes 4194304 | tf_op jit(solution)/shard_map/all_to_all | solution.py:40
  285.5 0.9 copy-start.17
  285.5 0.9 copy-start.18
  285.5 0.9 copy-start.19
  285.5 0.9 copy-start.26
  285.5 0.9 copy-start.27
  285.5 0.9 copy-start.28
  352.3 37.6 %all-to-all-start.3 = ((f32[16,2,2,8,1024]{4,3,1,2,0:T(8,128)}), f32[16,2,2,8,1024]{4,3,1,2,0:T(8,128)}, u32[]{:S(2)}, u32[]{:S(2)}) async-start(f32[16,2,2,8,1024]{4,3,1,2,0:T(8,128)} %bitcast.450), calls=%async_computation.3 | async-start | bytes 4194304 | tf_op jit(solution)/shard_map/all_to_all | solution.py:40
  358.4 12.7 %slice-start.2 = ((s8[6291456]{0:T(1024)(128)(4,1)}), s8[4194304]{0:T(1024)(128)(4,1)S(1)}, s32[]{:S(2)}) async-start(s8[6291456]{0:T(1024)(128)(4,1)} %bitcast.482), calls=%async_computation.9 | async-start | bytes 8388608
  358.4 12.7 %slice-start.3 = ((s8[6291456]{0:T(1024)(128)(4,1)}), s8[2097152]{0:T(1024)(128)(4,1)S(1)}, s32[]{:S(2)}) async-start(s8[6291456]{0:T(1024)(128)(4,1)} %bitcast.482), calls=%async_computation.10 | async-start | bytes 4194304
  384.8 12.5 %copy-start.11 = (f32[3,1,512]{2,0,1:T(4,128)S(1)}, f32[3,1,512]{2,0,1:T(4,128)}, u32[]{:S(2)}) copy-start(f32[3,1,512]{2,0,1:T(4,128)} %copy.137) | copy-start | bytes 18436
  384.8 12.5 %copy-start.12 = (f32[3,1,512]{2,0,1:T(4,128)S(1)}, f32[3,1,512]{2,0,1:T(4,128)}, u32[]{:S(2)}) copy-start(f32[3,1,512]{2,0,1:T(4,128)} %copy.138) | copy-start | bytes 18436
  384.8 12.5 %copy-start.13 = (f32[3,1,512]{2,0,1:T(4,128)S(1)}, f32[3,1,512]{2,0,1:T(4,128)}, u32[]{:S(2)}) copy-start(f32[3,1,512]{2,0,1:T(4,128)} %copy.139) | copy-start | bytes 18436
  384.8 12.5 %copy-start.14 = (f32[3,1,512]{2,0,1:T(4,128)S(1)}, f32[3,1,512]{2,0,1:T(4,128)}, u32[]{:S(2)}) copy-start(f32[3,1,512]{2,0,1:T(4,128)} %copy.140) | copy-start | bytes 18436
  384.8 12.5 %copy-start.15 = (f32[3,1,512]{2,0,1:T(4,128)S(1)}, f32[3,1,512]{2,0,1:T(4,128)}, u32[]{:S(2)}) copy-start(f32[3,1,512]{2,0,1:T(4,128)} %copy.141) | copy-start | bytes 18436
  384.8 12.5 %copy-start.16 = (f32[3,1,512]{2,0,1:T(4,128)S(1)}, f32[3,1,512]{2,0,1:T(4,128)}, u32[]{:S(2)}) copy-start(f32[3,1,512]{2,0,1:T(4,128)} %copy.142) | copy-start | bytes 18436
  389.9 36.5 %all-to-all-start.4 = ((f32[16,2,2,8,1024]{4,3,1,2,0:T(8,128)}), f32[16,2,2,8,1024]{4,3,1,2,0:T(8,128)S(1)}, u32[]{:S(2)}, u32[]{:S(2)}) async-start(f32[16,2,2,8,1024]{4,3,1,2,0:T(8,128)} %bitcast.490), calls=%async_computation.4 | async-start | bytes 4194304 | tf_op jit(solution)/shard_map/all_to_all | solution.py:40
  397.4 8.5 %copy-start.5 = (bf16[1,2,128,3,2,512]{5,2,4,3,1,0:T(8,128)(2,1)S(1)}, bf16[1,2,128,3,2,512]{5,2,4,3,1,0:T(8,128)(2,1)}, u32[]{:S(2)}) copy-start(bf16[1,2,128,3,2,512]{5,2,4,3,1,0:T(8,128)(2,1)} %get-tuple-element.94) | copy-start | bytes 4718596
  397.4 8.5 %copy-start.9 = (bf16[1,2,128,3,2,512]{5,2,4,3,1,0:T(8,128)(2,1)S(1)}, bf16[1,2,128,3,2,512]{5,2,4,3,1,0:T(8,128)(2,1)}, u32[]{:S(2)}) copy-start(bf16[1,2,128,3,2,512]{5,2,4,3,1,0:T(8,128)(2,1)} %get-tuple-element.95) | copy-start | bytes 4718596
  397.4 13.4 %slice-start.6 = ((s8[9437184]{0:T(1024)(128)(4,1)}), s8[4194304]{0:T(1024)(128)(4,1)S(1)}, s32[]{:S(2)}) async-start(s8[9437184]{0:T(1024)(128)(4,1)} %bitcast.486), calls=%async_computation.13 | async-start | bytes 8388608
  405.8 4.9 slice-start.7
  405.8 4.9 slice-start.8
  411.3 20.1 %copy-start.20 = (f32[3,512]{1,0:T(4,128)S(1)}, f32[3,512]{1,0:T(4,128)}, u32[]{:S(2)}) copy-start(f32[3,512]{1,0:T(4,128)} %get-tuple-element.116) | copy-start | bytes 18436
  411.3 20.1 %copy-start.21 = (f32[3,512]{1,0:T(4,128)S(1)}, f32[3,512]{1,0:T(4,128)}, u32[]{:S(2)}) copy-start(f32[3,512]{1,0:T(4,128)} %get-tuple-element.117) | copy-start | bytes 18436
  411.3 20.1 %copy-start.22 = (f32[3,512]{1,0:T(4,128)S(1)}, f32[3,512]{1,0:T(4,128)}, u32[]{:S(2)}) copy-start(f32[3,512]{1,0:T(4,128)} %get-tuple-element.118) | copy-start | bytes 18436
  411.3 20.1 %copy-start.23 = (f32[3,512]{1,0:T(4,128)S(1)}, f32[3,512]{1,0:T(4,128)}, u32[]{:S(2)}) copy-start(f32[3,512]{1,0:T(4,128)} %get-tuple-element.113) | copy-start | bytes 18436
  411.3 20.1 %copy-start.24 = (f32[3,512]{1,0:T(4,128)S(1)}, f32[3,512]{1,0:T(4,128)}, u32[]{:S(2)}) copy-start(f32[3,512]{1,0:T(4,128)} %get-tuple-element.114) | copy-start | bytes 18436
  411.3 20.1 %copy-start.25 = (f32[3,512]{1,0:T(4,128)S(1)}, f32[3,512]{1,0:T(4,128)}, u32[]{:S(2)}) copy-start(f32[3,512]{1,0:T(4,128)} %get-tuple-element.115) | copy-start | bytes 18436
  426.5 34.2 %all-to-all-start.2 = ((f32[16,2,2,8,1024]{4,3,1,2,0:T(8,128)}), f32[16,2,2,8,1024]{4,3,1,2,0:T(8,128)}, u32[]{:S(2)}, u32[]{:S(2)}) async-start(f32[16,2,2,8,1024]{4,3,1,2,0:T(8,128)} %bitcast.491), calls=%async_computation.2 | async-start | bytes 4194304 | tf_op jit(solution)/shard_map/all_to_all | solution.py:40
  431.5 7.8 %copy-start.6 = (bf16[1,2,128,3,2,512]{5,2,4,3,1,0:T(8,128)(2,1)S(1)}, bf16[1,2,128,3,2,512]{5,2,4,3,1,0:T(8,128)(2,1)}, u32[]{:S(2)}) copy-start(bf16[1,2,128,3,2,512]{5,2,4,3,1,0:T(8,128)(2,1)} %get-tuple-element.94) | copy-start | bytes 4718596
  431.5 7.8 %copy-start.10 = (bf16[1,2,128,3,2,512]{5,2,4,3,1,0:T(8,128)(2,1)S(1)}, bf16[1,2,128,3,2,512]{5,2,4,3,1,0:T(8,128)(2,1)}, u32[]{:S(2)}) copy-start(bf16[1,2,128,3,2,512]{5,2,4,3,1,0:T(8,128)(2,1)} %get-tuple-element.95) | copy-start | bytes 4718596
  460.7 34.2 %all-to-all-start.5 = ((f32[16,2,2,8,1024]{4,3,1,2,0:T(8,128)}), f32[16,2,2,8,1024]{4,3,1,2,0:T(8,128)}, u32[]{:S(2)}, u32[]{:S(2)}) async-start(f32[16,2,2,8,1024]{4,3,1,2,0:T(8,128)} %bitcast.492), calls=%async_computation.5 | async-start | bytes 4194304 | tf_op jit(solution)/shard_map/all_to_all | solution.py:40
  469.2 28.8 %copy-start.29 = (s32[6]{0:T(128)S(1)}, s32[6]{0:T(128)}, u32[]{:S(2)}) copy-start(s32[6]{0:T(128)} %param.6) | copy-start | bytes 76
Sparse Core Ops, SparseCore 0:
  9.0 131.5 all-gather.1
where the time goes:
time: 511 us; the launch traced here: 507 us
  waiting for transfers between devices  227 us (44%)
  other arithmetic  106 us (21%)
  local copies, waits for them, and re-layouts  91.6 us (18%)
  starting transfers between devices  41.3 us (8%)
  matrix products  26.5 us (5%)
  between operations  14.7 us (3%)
    all_gather x1, waiting for transfers between devices, on_device(): gathered = lax.all_gather(vectors, 'vec', axis=0, tiled=True)  119 us
    all_to_all x6, waiting for transfers between devices, sum_at_owner(): lax.all_to_all(blocks, axis, split_axis=0, concat_axis=0, tiled=True)  107 us
    convert_element_type x6, other arithmetic, displace(): disp_real.astype(jnp.bfloat16)  37.8 us
    all_to_all x6, starting transfers between devices, sum_at_owner(): lax.all_to_all(blocks, axis, split_axis=0, concat_axis=0, tiled=True)  35.9 us
    select_n x2, other arithmetic, neighbour(): return jnp.where(position == extent - 1, beside_all, inside)  34.9 us
    dot_general x6, matrix products, on_device(): jnp.einsum('qpicrs,jcrs->pqij', left_side, displaced, preferred_element_t...  25.9 us
    slice x8, local copies, waits for them, and re-layouts, neighbour(): beside_all = jnp.roll(field, -(extent - 1) * stride, axis=-1)  24.6 us
    mul x10, other arithmetic, colour_apply(): out_real = out_real + left_real * right_real - left_imag * right_imag  19 us
  transfers between devices with their start and end apart: 10, of which 6 were waited for; matrix products, arithmetic and copies ran while one was open for 33% of the time, Pallas kernels for 0%

commit v1 on v0

v1 whole, which is shorter than its diff:
```python
import math

import jax
import jax.numpy as jnp
from jax import lax
from jax.sharding import PartitionSpec as P

LX = 32
LY = 8


def colour_apply(link_real, link_imag, vec_real, vec_imag):
    out_real = jnp.float32(0.0)
    out_imag = jnp.float32(0.0)
    for column in range(3):
        left_real = link_real[None, :, column]
        left_imag = link_imag[None, :, column]
        right_real = vec_real[:, None, column].astype(jnp.float32)
        right_imag = vec_imag[:, None, column].astype(jnp.float32)
        out_real = out_real + left_real * right_real - left_imag * right_imag
        out_imag = out_imag + left_real * right_imag + left_imag * right_real
    return (out_real, out_imag)


def neighbour(field, stride, extent, position, forward):
    if forward:
        inside = jnp.roll(field, -stride, axis=-1)
        beside_all = jnp.roll(field, (extent - 1) * stride, axis=-1)
        return jnp.where(position == extent - 1, beside_all, inside)
    inside = jnp.roll(field, stride, axis=-1)
    beside_all = jnp.roll(field, -(extent - 1) * stride, axis=-1)
    return jnp.where(position == 0, beside_all, inside)


def on_device(vectors, links, dirs, moms):
    sites = vectors.shape[-1]
    plane = LY * LX
    depth = sites // plane
    shards = lax.axis_size("gz")
    flat = jnp.arange(sites, dtype=jnp.int32)
    x_index = flat % LX
    y_index = flat // LX % LY
    z_index = lax.axis_index("gz") * depth + flat // plane
    up = [(i, (i + 1) % shards) for i in range(shards)]
    down = [((i + 1) % shards, i) for i in range(shards)]
    gathered = lax.all_gather(vectors, "vec", axis=0, tiled=True)
    lower_links = lax.ppermute(links[2, :, :, :, sites - plane :], "gz", up)
    below = lax.ppermute(vectors[..., sites - plane :], "gz", up)
    above = lax.ppermute(vectors[..., :plane], "gz", down)
    momenta = moms.astype(jnp.float32)
    terms = []
    for direction in range(6):
        axis = direction % 3
        back = direction < 3
        step = -1 if back else 1
        link = links[axis]
        if axis == 0:
            moved = neighbour(vectors, 1, LX, x_index, not back)
            beside = neighbour(link, 1, LX, x_index, False) if back else link
        elif axis == 1:
            moved = neighbour(vectors, LX, LY, y_index, not back)
            beside = neighbour(link, LX, LY, y_index, False) if back else link
        elif back:
            moved = jnp.concatenate((below, vectors[..., : sites - plane]), axis=-1)
            beside = jnp.concatenate((lower_links, link[..., : sites - plane]), axis=-1)
        else:
            moved = jnp.concatenate((vectors[..., plane:], above), axis=-1)
            beside = link
        if back:
            link_real = jnp.swapaxes(beside[:, :, 0], 0, 1)
            link_imag = -jnp.swapaxes(beside[:, :, 1], 0, 1)
        else:
            link_real = beside[:, :, 0]
            link_imag = beside[:, :, 1]
        real, imag = colour_apply(link_real, link_imag, moved[:, :, 0], moved[:, :, 1])
        theta = (
            momenta[:, 0, None] * (x_index + (step if axis == 0 else 0)).astype(jnp.float32) / LX
            + momenta[:, 1, None] * (y_index + (step if axis == 1 else 0)).astype(jnp.float32) / LY
            + momenta[:, 2, None] * (z_index + (step if axis == 2 else 0)).astype(jnp.float32) / (depth * shards)
        ) * (2.0 * math.pi)
        cosine = jnp.cos(theta)[:, None, None]
        sine = jnp.sin(theta)[:, None, None]
        left_real = (cosine * real - sine * imag).astype(jnp.bfloat16)
        left_imag = (sine * real + cosine * imag).astype(jnp.bfloat16)
        left = jnp.stack(
            (
                jnp.stack((left_real, left_imag), axis=3),
                jnp.stack((-left_imag, left_real), axis=3),
            ),
            axis=0,
        )
        product = jnp.einsum("qpicrs,jcrs->pqij", left, gathered, preferred_element_type=jnp.float32)
        terms.append(lax.psum_scatter(product, "gz", scatter_dimension=2, tiled=True))
    stacked = jnp.stack(terms, axis=0)
    select = (dirs[:, None] == jnp.arange(6, dtype=jnp.int32)[None, :]).astype(jnp.float32)
    chosen = jnp.einsum("dk,kpqij->dpqij", select, stacked, precision=lax.Precision.HIGHEST)
    return chosen * (1.0 / math.sqrt(3.0 * sites * shards))


def solution(mesh):
    placed = (P("vec", None, None, "gz"), P(None, None, None, None, "gz"), P(), P())
    return jax.shard_map(
        on_device,
        mesh=mesh,
        in_specs=placed,
        out_specs=P(None, None, None, ("vec", "gz"), None),
        check_vma=False,
    )
```

time: 511 us -> 601 us (1.18)
  waiting for transfers between devices: 227 us -> 495 us
  other arithmetic: 106 us -> 16.4 us
  local copies, waits for them, and re-layouts: 91.6 us -> 32.3 us
  starting transfers between devices: 41.3 us -> 9.11 us
  matrix products: 26.5 us -> 32.9 us
    reduce_scatter x0 -> x6, waiting for transfers between devices: none -> 378 us  [on_device(): lax.psum_scatter(product, 'gz', scatter_dimension=2, tiled=True)]
    all_to_all x6 -> x0, waiting for transfers between devices: 107 us -> none  [sum_at_owner(): lax.all_to_all(blocks, axis, split_axis=0, concat_axis=0, tiled=True)]
    convert_element_type x10 -> x11, other arithmetic: 40.4 us -> 1.71 us  [the longest x6 1.67 us: on_device(): left_real = (cosine * real - sine * imag).astype(jnp.bfloat16)]
    all_to_all x6 -> x0, starting transfers between devices: 35.9 us -> none  [sum_at_owner(): lax.all_to_all(blocks, axis, split_axis=0, concat_axis=0, tiled=True)]
    select_n x2 -> x0, other arithmetic: 34.9 us -> none  [neighbour(): return jnp.where(position == extent - 1, beside_all, inside)]
    slice x8 -> x4, local copies, waits for them, and re-layouts: 24.6 us -> 1.42 us  [neighbour(): beside_all = jnp.roll(field, -(extent - 1) * stride, axis=-1)]
    mul x10, other arithmetic: 19 us -> 0.95 us  [colour_apply(): out_real = out_real + left_real * right_real - left_imag * right_imag]
    slice x6 -> x2, local copies, waits for them, and re-layouts: 15.9 us -> 0.75 us  [neighbour(): inside = jnp.roll(field, stride, axis=-1)]
  transfers between devices with their start and end apart: 10 -> 10, of which waited for: 6 -> 8; matrix products, arithmetic and copies ran while one was open for 33% -> 11% of each run, Pallas kernels for 0% -> 0%
where the time goes in v1:
time: 601 us; the launch traced here: 600 us
  waiting for transfers between devices  495 us (82%)
  matrix products  32.9 us (5%)
  local copies, waits for them, and re-layouts  32.3 us (5%)
  other arithmetic  16.4 us (3%)
  between operations  14.6 us (2%)
  starting transfers between devices  9.11 us (2%)
    reduce_scatter x6, waiting for transfers between devices, on_device(): lax.psum_scatter(product, 'gz', scatter_dimension=2, tiled=True)  378 us
    all_gather x1, waiting for transfers between devices, on_device(): gathered = lax.all_gather(vectors, 'vec', axis=0, tiled=True)  111 us
    dot_general x6, matrix products, on_device(): jnp.einsum('qpicrs,jcrs->pqij', left, gathered, preferred_element_type=jn...  31.9 us
    unnamed x111, local copies, waits for them, and re-layouts  18.3 us
  transfers between devices with their start and end apart: 10, of which 8 were waited for; matrix products, arithmetic and copies ran while one was open for 11% of the time, Pallas kernels for 0%

profile of v1, /device:TPU:0, one launch (start us, length us, event | category | flops | bytes accessed | tf_op | source)
XLA Modules:
  0.0 600.4 jit_solution(9777820009141862032)
XLA Ops:
  6.5 2.1 copy.8
  8.7 2.0 fusion.148
  10.7 0.6 slice_bitcast_fusion.47
  11.3 4.1 collective-permute-start
  15.4 0.6 slice_bitcast_fusion.44
  16.0 0.7 slice.588
  16.7 0.6 slice.589
  17.3 0.7 slice.590
  18.5 1.0 fusion.129
  20.0 0.4 fusion.144
  20.4 0.4 fusion.147
  20.8 1.4 maximum_select_fusion
  22.4 0.6 multiply_subtract_fusion.5
  23.7 1.4 maximum_bitcast_fusion
  25.2 0.6 copy_bitcast_fusion.8
  25.9 0.7 fusion.149
  27.5 1.3 maximum_select_fusion.1
  28.8 1.0 slice_bitcast_fusion.5
  29.8 110.8 %all-gather.2.cloned.1.call-done = bf16[1024,3,2,512]{3,0,2,1:T(8,128)(2,1)} async-done(((bf16[128,3,2,512]{3,0,2,1:T(8,128)(2,1)}), bf16[1024,3,2,512]{3,0,2,1:T(8,128)(2,1)}) %all-gather.2.cloned.1.call-update) | async-done | bytes 6291472 | tf_op jit(solution)/shard_map/all_gather | solution.py:46
  140.6 8.1 %fusion.30 = f32[2,2,128,1024]{3,2,0,1:T(8,128)} fusion(bf16[1024,3,2,512]{3,0,2,1:T(8,128)(2,1)} %all-gather.2.cloned.1.call-done, bf16[1,2,128,3,2,512]{5,2,4,3,1,0:T(8,128)(2,1)} %get-tuple-element.83, bf16[1,2,128,3,2,512]{5,2,4,3,1,0:T(8,128)(2,1)S(1)} %get-tuple-element.82), kind=kOutput, calls=%fused_computation.30 | convolution fusion | flops 3222798336 | bytes 11534336 | tf_op jit(solution)/shard_map/qpicrs,jcrs->pqij/dot_general | solution.py:92
  149.0 0.4 copy-done.13
  149.4 0.6 slice.612
  150.0 0.6 copy.101
  150.7 0.7 sin.44
  151.6 0.6 multiply_subtract_fusion.4
  153.1 1.0 copy-done.5
  154.2 0.6 slice-done.1
  154.7 4.7 fusion.35
  159.6 0.6 copy-done.20
  160.2 0.8 fusion.103
  161.1 1.1 fusion.64
  162.4 0.6 multiply_subtract_fusion.3
  163.9 0.8 slice-done.2
  164.7 1.0 slice-done.3
  165.6 4.8 fusion.40
  171.4 0.6 multiply_subtract_fusion.2
  172.9 0.8 slice-done.4
  173.6 0.9 slice-done.5
  174.5 4.8 fusion.45
  179.4 0.7 copy-done.14
  180.5 0.6 multiply_subtract_fusion.1
  181.9 0.8 slice-done.6
  182.7 1.2 slice-done.7
  183.9 4.8 fusion.50
  188.7 4.4 collective-permute-start.2
  193.3 6.1 %collective-permute-done.2 = bf16[128,3,2,256]{3,0,2,1:T(8,128)(2,1)S(1)} collective-permute-done((bf16[128,3,2,256]{3,0,2,1:T(8,128)(2,1)S(1)}, bf16[128,3,2,256]{3,0,2,1:T(8,128)(2,1)S(1)}, u32[]{:S(2)}, u32[]{:S(2)}) %collective-permute-start.2) | collective-permute-done | bytes 393248 | tf_op jit(solution)/shard_map/ppermute | solution.py:49
  199.7 0.6 multiply_subtract_fusion
  201.1 0.8 slice-done.8
  201.9 0.9 slice-done.9
  202.8 4.7 fusion.55
  207.6 13.6 %reduce-scatter.7.cloned.1.call-done = f32[2,2,8,1024]{3,2,0,1:T(8,128)} async-done(((f32[2,2,128,1024]{3,2,0,1:T(8,128)}), f32[2,2,8,1024]{3,2,0,1:T(8,128)}) %reduce-scatter.7.cloned.1.call-update) | async-done | bytes 131088 | tf_op jit(solution)/shard_map/reduce_scatter | solution.py:93
  221.2 0.9 bitcast_dynamic-update-slice_fusion.5
  222.1 73.0 %reduce-scatter.9.cloned.1.call-done = f32[2,2,8,1024]{3,2,0,1:T(8,128)} async-done(((f32[2,2,128,1024]{3,2,0,1:T(8,128)}), f32[2,2,8,1024]{3,2,0,1:T(8,128)}) %reduce-scatter.9.cloned.1.call-update) | async-done | bytes 131088 | tf_op jit(solution)/shard_map/reduce_scatter | solution.py:93
  295.1 0.9 bitcast_dynamic-update-slice_fusion.4
  296.0 72.8 %reduce-scatter.11.cloned.1.call-done = f32[2,2,8,1024]{3,2,0,1:T(8,128)} async-done(((f32[2,2,128,1024]{3,2,0,1:T(8,128)}), f32[2,2,8,1024]{3,2,0,1:T(8,128)}) %reduce-scatter.11.cloned.1.call-update) | async-done | bytes 131088 | tf_op jit(solution)/shard_map/reduce_scatter | solution.py:93
  368.9 0.9 bitcast_dynamic-update-slice_fusion.3
  369.8 72.8 %reduce-scatter.13.cloned.1.call-done = f32[2,2,8,1024]{3,2,0,1:T(8,128)} async-done(((f32[2,2,128,1024]{3,2,0,1:T(8,128)}), f32[2,2,8,1024]{3,2,0,1:T(8,128)}) %reduce-scatter.13.cloned.1.call-update) | async-done | bytes 131088 | tf_op jit(solution)/shard_map/reduce_scatter | solution.py:93
  442.6 0.9 bitcast_dynamic-update-slice_fusion.2
  443.5 72.8 %reduce-scatter.15.cloned.1.call-done = f32[2,2,8,1024]{3,2,0,1:T(8,128)} async-done(((f32[2,2,128,1024]{3,2,0,1:T(8,128)}), f32[2,2,8,1024]{3,2,0,1:T(8,128)}) %reduce-scatter.15.cloned.1.call-update) | async-done | bytes 131088 | tf_op jit(solution)/shard_map/reduce_scatter | solution.py:93
  516.4 0.9 bitcast_dynamic-update-slice_fusion.1
  517.3 73.0 %reduce-scatter.17.cloned.1.call-done = f32[2,2,8,1024]{3,2,0,1:T(8,128)} async-done(((f32[2,2,128,1024]{3,2,0,1:T(8,128)}), f32[2,2,8,1024]{3,2,0,1:T(8,128)}) %reduce-scatter.17.cloned.1.call-update) | async-done | bytes 131088 | tf_op jit(solution)/shard_map/reduce_scatter | solution.py:93
  590.2 0.9 bitcast_dynamic-update-slice_fusion
  591.2 1.0 convolution_multiply_fusion
  592.2 1.3 copy.28
  (188 shorter events, 9.8 us)
Async XLA Ops:
  6.5 134.0 %all-gather.2.cloned.1.call-start = ((), (), s32[]{:S(2)}) async-start(), calls=%async_computation.6 | async-start | bytes 7077888 | tf_op jit(solution)/shard_map/all_gather | solution.py:46
  8.6 2.1 copy-start.10
  8.6 9.6 %copy-start.29 = (s32[2,3]{1,0:T(2,128)S(1)}, s32[2,3]{1,0:T(2,128)}, u32[]{:S(2)}) copy-start(s32[2,3]{1,0:T(2,128)} %param.7) | copy-start | bytes 76
  8.6 11.1 %copy-start = (bf16[128,3,2,512]{3,0,2,1:T(8,128)(2,1)S(1)}, bf16[128,3,2,512]{3,0,2,1:T(8,128)(2,1)}, u32[]{:S(2)}) copy-start(bf16[128,3,2,512]{3,0,2,1:T(8,128)(2,1)} %copy.8) | copy-start | bytes 2359300
  8.7 212.5 %reduce-scatter.7.cloned.1.call-start = ((), (), s32[]{:S(2)}) async-start(), calls=%async_computation.7 | async-start | bytes 2228224 | tf_op jit(solution)/shard_map/reduce_scatter | solution.py:93
  10.7 150.4 %collective-permute-start.1 = (bf16[128,3,2,256]{3,0,2,1:T(8,128)(2,1)S(1)}, bf16[128,3,2,256]{3,0,2,1:T(8,128)(2,1)}, u32[]{:S(2)}, u32[]{:S(2)}) collective-permute-start(bf16[128,3,2,256]{3,0,2,1:T(8,128)(2,1)S(1)} %get-tuple-element.76), channel_id=1, source_target_pairs={{0,1},{1,2},{2,3},{3,4},{4,5},{5,6},{6,7},{7,8},{8,9},{9,10},{10,1... | collective-permute-start | bytes 1179656 | tf_op jit(solution)/shard_map/ppermute | solution.py:48
  11.3 148.2 %collective-permute-start = (f32[3,3,2,256]{3,2,1,0:T(2,128)}, f32[3,3,2,256]{3,2,1,0:T(2,128)}, u32[]{:S(2)}, u32[]{:S(2)}) collective-permute-start(f32[3,3,2,256]{3,2,1,0:T(2,128)} %slice_bitcast_fusion.47), channel_id=1, source_target_pairs={{0,1},{1,2},{2,3},{3,4},{4,5},{5,6},{6,7},{7,8},{8,9},{9,10},{10,1... | collective-permute-start | bytes 55304 | tf_op jit(solution)/shard_map/ppermute | solution.py:47
  16.0 4.4 copy-start.4
  16.0 4.4 copy-start.6
  23.6 1.4 copy-start.7
  23.6 1.4 copy-start.11
  23.6 1.4 copy-start.19
  23.6 1.4 copy-start.23
  23.7 2.2 copy-start.8
  148.7 0.7 copy-start.13
  148.7 0.8 copy-start.9
  148.7 1.4 copy-start.18
  148.7 2.0 copy-start.28
  148.7 2.7 copy-start.27
  148.7 2.7 copy-start.12
  148.7 2.7 copy-start.3
  148.7 2.8 copy-start.2
  148.7 146.4 %reduce-scatter.9.cloned.1.call-start = ((), (), s32[]{:S(2)}) async-start(), calls=%async_computation.8 | async-start | bytes 2228224 | tf_op jit(solution)/shard_map/reduce_scatter | solution.py:93
  151.6 0.7 copy-start.21
  151.6 2.6 slice-start
  152.6 2.2 slice-start.1
  152.9 1.2 copy-start.5
  159.5 0.7 copy-start.20
  159.5 1.6 copy-start.1
  159.5 209.4 %reduce-scatter.11.cloned.1.call-start = ((), (), s32[]{:S(2)}) async-start(), calls=%async_computation.9 | async-start | bytes 2228224 | tf_op jit(solution)/shard_map/reduce_scatter | solution.py:93
  162.4 0.7 copy-start.22
  162.4 2.3 slice-start.2
  163.3 2.3 slice-start.3
  170.4 0.7 copy-start.26
  170.5 272.1 %reduce-scatter.13.cloned.1.call-start = ((), (), s32[]{:S(2)}) async-start(), calls=%async_computation.10 | async-start | bytes 2228224 | tf_op jit(solution)/shard_map/reduce_scatter | solution.py:93
  171.4 2.2 slice-start.4
  172.3 2.2 slice-start.5
  179.3 0.7 copy-start.14
  179.3 0.8 copy-start.17
  179.3 0.9 copy-start.25
  179.3 337.0 %reduce-scatter.15.cloned.1.call-start = ((), (), s32[]{:S(2)}) async-start(), calls=%async_computation.11 | async-start | bytes 2228224 | tf_op jit(solution)/shard_map/reduce_scatter | solution.py:93
  180.5 2.2 slice-start.6
  181.4 2.5 slice-start.7
  188.6 4.4 copy-start.16
  188.6 4.5 copy-start.15
  188.6 4.6 copy-start.24
  188.7 401.6 %reduce-scatter.17.cloned.1.call-start = ((), (), s32[]{:S(2)}) async-start(), calls=%async_computation.12 | async-start | bytes 2228224 | tf_op jit(solution)/shard_map/reduce_scatter | solution.py:93
  188.7 10.7 %collective-permute-start.2 = (bf16[128,3,2,256]{3,0,2,1:T(8,128)(2,1)S(1)}, bf16[128,3,2,256]{3,0,2,1:T(8,128)(2,1)S(1)}, u32[]{:S(2)}, u32[]{:S(2)}) collective-permute-start(bf16[128,3,2,256]{3,0,2,1:T(8,128)(2,1)S(1)} %copy-done.1), channel_id=1, source_target_pairs={{1,0},{2,1},{3,2},{4,3},{5,4},{6,5},{7,6},{8,7},{9,8},{10,9},{11,1... | collective-permute-start | bytes 1179656 | tf_op jit(solution)/shard_map/ppermute | solution.py:49
  199.7 2.2 slice-start.8
  200.6 2.2 slice-start.9
  207.5 383.6 %copy-start.30 = (s32[6]{0:T(128)S(1)}, s32[6]{0:T(128)}, u32[]{:S(2)}) copy-start(s32[6]{0:T(128)} %param.6) | copy-start | bytes 76
Sparse Core Ops, SparseCore 0:
  9.0 131.5 all-gather.1
  148.8 72.2 reduce-scatter.6
  225.1 69.9 reduce-scatter.8
  298.9 69.9 reduce-scatter.10
  372.7 69.9 reduce-scatter.12
  446.4 69.9 reduce-scatter.14
  520.3 69.8 reduce-scatter.16

commit v2 on v1

v2 whole, which is shorter than its diff:
```python
import functools
import math

import jax
import jax.numpy as jnp
from jax import lax
from jax.experimental import pallas as pl
from jax.experimental.pallas import tpu as pltpu
from jax.sharding import PartitionSpec as P

LX = 32
LY = 8
PLANE = LX * LY
F32 = jnp.float32
BF16 = jnp.bfloat16
MESH = pl.DeviceIdType.MESH
NT = (((1,), (1,)), ((), ()))


def lanes(start, size, multiple=128):
    return pl.ds(pl.multiple_of(start, multiple), size)


def shifted(a, b, lane, kind):
    if kind == 0:
        first = lane % LX == 0
        return [jnp.where(first, pltpu.roll(v, 97, 1), pltpu.roll(v, 1, 1)) for v in (a, b)]
    if kind == 2:
        last = lane % LX == LX - 1
        return [jnp.where(last, pltpu.roll(v, 31, 1), pltpu.roll(v, 127, 1)) for v in (a, b)]
    if kind == 1:
        first = lane < LX
        ra, rb = pltpu.roll(a, 32, 1), pltpu.roll(b, 32, 1)
        return [jnp.where(first, rb, ra), jnp.where(first, ra, rb)]
    last = lane >= 96
    ra, rb = pltpu.roll(a, 96, 1), pltpu.roll(b, 96, 1)
    return [jnp.where(last, rb, ra), jnp.where(last, ra, rb)]


def kernel(
    v_ref, u_ref, dirs_ref, moms_ref, o_ref,
    V, A, RE, IM, XF, XS, LK, LS, LKR, LHR, PC, PS, HS, HB,
    S1, R1, S2, R2, T, R4, FS,
    ss_own, ss_f01, ss_half, ss_z, ss_core, rs_ag, rs_core,
    ss_link, rs_link, ss_halo, rs_halo, ss_lh, rs_lh,
    ss_1, rs_1, ss_2, rs_2, ss_4, rs_4,
):
    v = lax.axis_index("vec")
    g = lax.axis_index("gz")
    y, zl = v // 2, v % 2
    x, zh, core = g // 4, (g // 2) % 2, g % 2
    chip = g // 2
    other = 1 - core

    def at(yy, zz):
        return ((yy + 8) % 4) * 2 + zz

    dev_core = (v, chip * 2 + other)
    dev_yp = (at(y + 1, zl), g)
    dev_ym = (at(y - 1, zl), g)
    dev_z = (y * 2 + (1 - zl), g)
    dev_xp = (v, (((x + 1) % 4) * 2 + zh) * 2 + core)
    dev_xm = (v, (((x + 3) % 4) * 2 + zh) * 2 + core)
    dev_zh = (v, (x * 2 + (1 - zh)) * 2 + core)
    up = (chip + 1) % 8
    down = (chip + 7) % 8
    barrier = pltpu.get_barrier_semaphore()
    everyone = [dev_core, dev_yp, dev_ym, dev_z, dev_xp, dev_xm, dev_zh]
    everyone += [(v, up * 2), (v, up * 2 + 1), (v, down * 2), (v, down * 2 + 1)]
    for dev in everyone:
        pl.semaphore_signal(barrier, inc=1, device_id=dev, device_id_type=MESH)
    pl.semaphore_wait(barrier, len(everyone))

    def copy(src, dst, ss, rs, dev):
        return pltpu.make_async_remote_copy(
            src_ref=src, dst_ref=dst, send_sem=ss, recv_sem=rs, device_id=dev, device_id_type=MESH
        )

    def own_copies(c):
        return [
            copy(v_ref.at[c], V.at[core, 0, c], ss_own.at[0, c], rs_core.at[0, c], dev_core),
            copy(v_ref.at[c], V.at[core, 3, c], ss_own.at[1, c], rs_ag.at[3, c, 0], dev_yp),
            copy(v_ref.at[c], V.at[core, 2, c], ss_own.at[2, c], rs_ag.at[2, c, 0], dev_ym),
            copy(v_ref.at[c], V.at[core, 1, c], ss_own.at[3, c], rs_ag.at[1, c, 0], dev_z),
        ]

    def core_copy(slot, c):
        block = V.at[core, slot, c]
        return copy(block, block, ss_core.at[slot, c], rs_core.at[slot, c], dev_core)

    def core_wait(slot, c):
        block = V.at[other, slot, c]
        copy(block, block, ss_core.at[slot, c], rs_core.at[slot, c], dev_core).wait_recv()

    def ag_wait(slot, c):
        block = V.at[core, slot, c]
        copy(block, block, ss_z.at[c], rs_ag.at[slot, c, 0], dev_z).wait_recv()

    def half_copies(c):
        low, high = pl.ds(0, 64), pl.ds(64, 64)
        return [
            copy(V.at[core, 2, c, low], V.at[core, 4, c, low], ss_half.at[0, c], rs_ag.at[4, c, 0], dev_ym),
            copy(V.at[core, 3, c, high], V.at[core, 4, c, high], ss_half.at[1, c], rs_ag.at[4, c, 1], dev_yp),
        ]

    def f01_copies(c):
        return [
            copy(V.at[core, 1, c], V.at[core, 7, c], ss_f01.at[0, c], rs_ag.at[7, c, 0], dev_yp),
            copy(V.at[core, 1, c], V.at[core, 6, c], ss_f01.at[1, c], rs_ag.at[6, c, 0], dev_ym),
        ]

    def z_copy(c):
        return copy(V.at[core, 4, c], V.at[core, 5, c], ss_z.at[c], rs_ag.at[5, c, 0], dev_z)

    link_copy = copy(u_ref, LKR, ss_link, rs_link, dev_core)
    side = jnp.where(core == 1, up, down)

    def halo_copies():
        pairs = []
        for half in range(2):
            dev = (v, side * 2 + half)
            pairs.append(copy(HS.at[half], HB.at[other], ss_halo.at[half], rs_halo.at[other], dev))
            pairs.append(
                copy(u_ref.at[2, :, lanes(core * PLANE, PLANE)], LHR.at[other], ss_lh.at[half], rs_lh.at[other], dev)
            )
        return pairs

    for c in range(3):
        for one in own_copies(c):
            one.start()
    link_copy.start()

    for c in range(3):
        for r in range(2):
            plane = v_ref[c, :, lanes(r * 512 + core * PLANE, PLANE)].astype(F32).reshape(8, 2, 8, PLANE)
            for half in range(2):
                HS[half, c * 2 + r] = plane[:, half].reshape(64, PLANE).astype(BF16)
    for one in halo_copies():
        one.start()

    for c in range(3):
        V[core, 0, c] = v_ref[c]

    def extract(h, source):
        def body(i, carry):
            c, r = i // 2, i % 2
            for t in range(8):
                rows = source(c, pl.ds(t * 16, 16), lanes(r * 512, 512)).astype(F32)
                XF[i, t * 8 : t * 8 + 8, lanes(PLANE + h * 512, 512)] = jnp.where(core == 0, rows[:8], rows[8:])
            return carry

        lax.fori_loop(0, 6, body, 0)

    extract(core, lambda c, rows, cols: v_ref[c, rows, cols])

    site = lax.broadcasted_iota(jnp.int32, (16, 1024), 1)
    row = lax.broadcasted_iota(jnp.int32, (16, 1024), 0)
    k_row, p_row = row // 2, row % 2
    step = jnp.where(k_row < 3, -1, 1)
    mu_row = k_row % 3
    xs = site % LX + jnp.where(mu_row == 0, step, 0)
    ys = site // LX % LY + jnp.where(mu_row == 1, step, 0)
    zs = chip * 4 + site // PLANE + jnp.where(mu_row == 2, step, 0)

    def mom(axis):
        return jnp.where(p_row == 0, moms_ref[0, axis], moms_ref[1, axis])

    turns = (mom(0) * xs + 4 * mom(1) * ys + mom(2) * zs) & 31
    theta = turns.astype(F32) * (2.0 * math.pi / 32)
    PC[...] = jnp.cos(theta)
    PS[...] = jnp.sin(theta)

    link_copy.wait_recv()
    for mu in range(3):
        LK[mu, :, lanes(PLANE + core * 512, 512)] = u_ref[mu]
        LK[mu, :, lanes(PLANE + other * 512, 512)] = LKR[mu]
    lane_u = lax.broadcasted_iota(jnp.int32, (18, 128), 1)
    for mu in range(2):
        for plane in range(4):
            start = PLANE * (plane + 1)
            pair = shifted(LK[mu, :, start : start + 128], LK[mu, :, start + 128 : start + 256], lane_u, mu)
            LS[mu, :, plane * PLANE : plane * PLANE + 128] = pair[0]
            LS[mu, :, plane * PLANE + 128 : plane * PLANE + 256] = pair[1]

    for c in range(3):
        core_wait(0, c)
    extract(other, lambda c, rows, cols: V[other, 0, c, rows, cols])

    lane_x = lax.broadcasted_iota(jnp.int32, (64, 128), 1)

    def shift_body(i, carry):
        comp, plane = i // 4, i % 4
        a = XF[comp, :, lanes((plane + 1) * PLANE, 128)]
        b = XF[comp, :, lanes((plane + 1) * PLANE + 128, 128)]
        for kind in range(4):
            pair = shifted(a, b, lane_x, kind)
            XS[kind, comp, :, lanes(plane * PLANE, 128)] = pair[0]
            XS[kind, comp, :, lanes(plane * PLANE + 128, 128)] = pair[1]
        return carry

    lax.fori_loop(0, 24, shift_body, 0)

    def left(k):
        mu, back = k % 3, k < 3

        def body(lb, carry):
            here = lanes(lb * 128, 128)
            h, spot = lb // 4, (lb % 4) * 128
            if k < 2:
                link = [[[LS[mu, pl.ds((a * 3 + b) * 2 + r, 1), here] for r in range(2)] for b in range(3)] for a in range(3)]
            else:
                there = lanes(lb * 128 + (0 if k == 2 else PLANE), 128)
                link = [[[LK[mu, pl.ds((a * 3 + b) * 2 + r, 1), there] for r in range(2)] for b in range(3)] for a in range(3)]
            cs = [PC[pl.ds(k * 2 + p, 1), here] for p in range(2)]
            sn = [PS[pl.ds(k * 2 + p, 1), here] for p in range(2)]
            for ib in range(4):
                rows = pl.ds(ib * 16, 16)
                if mu == 2:
                    there = lanes(lb * 128 + (0 if back else 2 * PLANE), 128)
                    vec = [[XF[b * 2 + r, rows, there] for r in range(2)] for b in range(3)]
                else:
                    kind = mu if back else mu + 2
                    vec = [[XS[kind, b * 2 + r, rows, here] for r in range(2)] for b in range(3)]
                for a in range(3):
                    real = imag = None
                    for b in range(3):
                        vr, vi = vec[b]
                        if back:
                            ur, ui = link[b][a]
                            one = ur * vr + ui * vi
                            two = ur * vi - ui * vr
                        else:
                            ur, ui = link[a][b]
                            one = ur * vr - ui * vi
                            two = ur * vi + ui * vr
                        real = one if real is None else real + one
                        imag = two if imag is None else imag + two
                    for p in range(2):
                        into = pl.ds((k * 2 + p) * 64 + ib * 16, 16)
                        A[h * 3 + a, into, lanes(spot, 128)] = (cs[p] * real - sn[p] * imag).astype(BF16)
                        A[h * 3 + a, into, lanes(spot + 512, 128)] = (sn[p] * real + cs[p] * imag).astype(BF16)
            return carry

        lax.fori_loop(0, 8, body, 0)

    left(0)
    left(1)
    left(3)
    left(4)
    for one in range(2):
        copy(HS.at[0], HB.at[one], ss_halo.at[0], rs_halo.at[one], dev_core).wait_recv()
        copy(LHR.at[one], LHR.at[one], ss_lh.at[0], rs_lh.at[one], dev_core).wait_recv()
    for comp in range(6):
        XF[comp, :, 0:PLANE] = HB[0, comp].astype(F32)
        XF[comp, :, 5 * PLANE : 6 * PLANE] = HB[1, comp].astype(F32)
    LK[2, :, 0:PLANE] = LHR[0]
    left(2)
    left(5)

    def early(c):
        for slot in (2, 3, 1):
            ag_wait(slot, c)
            core_copy(slot, c).start()
        for one in half_copies(c):
            one.start()

    early(0)
    early(1)

    def product(pair, c, h):
        a = A[h * 3 + c]
        w = V[h, pl.ds(pair * 2, 2), c].reshape(256, 1024)
        real = lax.dot_general(a, w, NT, preferred_element_type=F32)
        imag = lax.dot_general(a[:, :512], w[:, 512:], NT, preferred_element_type=F32)
        imag = imag - lax.dot_general(a[:, 512:], w[:, :512], NT, preferred_element_type=F32)
        real = real.reshape(12, 64, 256)
        imag = imag.reshape(12, 64, 256)
        fresh = jnp.logical_and(c == 0, h == core)

        @pl.when(fresh)
        def _():
            RE[pair] = real
            IM[pair] = imag

        @pl.when(jnp.logical_not(fresh))
        def _():
            RE[pair] += real
            IM[pair] += imag

    def rows_of(xx):
        return pl.ds(pl.multiple_of((xx % 4) * 16, 16), 16)

    def s1_copies(n):
        return [
            copy(S1.at[n, 0], R1.at[n, 0], ss_1.at[n, 0], rs_1.at[n, 0], dev_xp),
            copy(S1.at[n, 1], R1.at[n, 1], ss_1.at[n, 1], rs_1.at[n, 1], dev_xm),
        ]

    def s2_copies(n):
        return [
            copy(S2.at[n, 0], R2.at[n, 0], ss_2.at[n, 0], rs_2.at[n, 0], dev_xp),
            copy(S2.at[n, 1], R2.at[n, 1], ss_2.at[n, 1], rs_2.at[n, 1], dev_xm),
        ]

    def s4_copy(n):
        return copy(T.at[n, :, pl.ds(pl.multiple_of((1 - zh) * 8, 8), 8)], R4.at[n], ss_4.at[n], rs_4.at[n], dev_zh)

    def stage1(n):
        S1[n, 0] = RE[n, :, rows_of(x + 2)].astype(BF16)
        S1[n, 1] = IM[n, :, rows_of(x + 2)].astype(BF16)
        for one in s1_copies(n):
            one.start()

    def stage2(n):
        for one in s1_copies(n):
            one.wait_recv()
        S2[n, 0, 0:12] = (RE[n, :, rows_of(x + 1)] + R1[n, 0].astype(F32)).astype(BF16)
        S2[n, 0, 12:24] = IM[n, :, rows_of(x + 1)].astype(BF16)
        S2[n, 1, 0:12] = RE[n, :, rows_of(x + 3)].astype(BF16)
        S2[n, 1, 12:24] = (IM[n, :, rows_of(x + 3)] + R1[n, 1].astype(F32)).astype(BF16)
        for one in s2_copies(n):
            one.start()

    def stage3(n):
        for one in s2_copies(n):
            one.wait_recv()
        T[n, 0:12] = RE[n, :, rows_of(x)] + (R2[n, 0, 0:12].astype(F32) + R2[n, 1, 0:12].astype(F32))
        T[n, 12:24] = IM[n, :, rows_of(x)] + (R2[n, 0, 12:24].astype(F32) + R2[n, 1, 12:24].astype(F32))
        s4_copy(n).start()

    scale = 1.0 / math.sqrt(3.0 * 8192)

    def stage4(n):
        s4_copy(n).wait_recv()
        total = (T[n, :, pl.ds(pl.multiple_of(zh * 8, 8), 8)] + R4[n]) * scale
        total = total.reshape(2, 6, 2, 8, 256)
        for q in range(2):
            for k in range(6):
                FS[k, :, q] = total[q, k]
        dy0 = jnp.where(n == 0, 0, jnp.where(n == 2, 2, 1))
        dy1 = jnp.where(n == 0, 0, jnp.where(n == 2, 2, 3))
        z0 = jnp.where(n == 3, 1 - zl, zl)
        z1 = jnp.where(n == 1, zl, 1 - zl)
        col0 = at(y + dy0, z0) * 128
        col1 = at(y + dy1, z1) * 128
        for d in range(6):
            block = FS[dirs_ref[d]]
            o_ref[d, :, :, :, lanes(col0, 128)] = block[..., 0:128]
            o_ref[d, :, :, :, lanes(col1, 128)] = block[..., 128:256]

    def when_at(u, places, work):
        hit = functools.reduce(jnp.logical_or, [u == place for place in places])
        n = jnp.where(u == places[1], 1, jnp.where(u == places[2], 2, jnp.where(u == places[3], 3, 0)))

        @pl.when(hit)
        def _():
            work(n)

    def main(u, carry):
        pair = jnp.where(u < 6, u // 3, jnp.where(u < 8, 2, jnp.where(u == 9, 2, 3)))
        c = jnp.where(u < 6, u % 3, jnp.where(u < 8, u - 6, jnp.where(u == 8, 0, jnp.where(u == 9, 2, u - 9))))

        @pl.when(u == 2)
        def _():
            early(2)
            for cc in range(3):
                for one in f01_copies(cc):
                    one.start()

        @pl.when(jnp.logical_and(u >= 3, u < 6))
        def _():
            for one in half_copies(u - 3):
                one.wait_recv()
            z_copy(u - 3).start()
            core_copy(4, u - 3).start()

        @pl.when(jnp.logical_and(u >= 6, u < 12))
        def _():
            @pl.when(pair == 2)
            def _():
                ag_wait(5, c)
                core_copy(5, c).start()

            @pl.when(pair == 3)
            def _():
                for slot in (6, 7):
                    ag_wait(slot, c)
                    core_copy(slot, c).start()

        when_at(u, (3, 6, 10, 12), stage1)
        when_at(u, (5, 8, 12, 13), stage2)
        when_at(u, (8, 11, 13, 14), stage3)
        when_at(u, (11, 13, 14, 15), stage4)

        @pl.when(u < 12)
        def _():
            def both(hh, carry2):
                h = jnp.where(hh == 0, core, other)

                @pl.when(hh == 1)
                def _():
                    core_wait(pair * 2 + 1, c)

                    @pl.when(pair > 0)
                    def _():
                        core_wait(pair * 2, c)

                product(pair, c, h)
                return carry2

            lax.fori_loop(0, 2, both, 0)

        return carry

    lax.fori_loop(0, 16, main, 0)

    for c in range(3):
        for one in own_copies(c) + half_copies(c) + f01_copies(c) + [z_copy(c)]:
            one.wait_send()
        for slot in range(1, 8):
            core_copy(slot, c).wait_send()
    link_copy.wait_send()
    for one in halo_copies():
        one.wait_send()
    for n in range(4):
        for one in s1_copies(n) + s2_copies(n) + [s4_copy(n)]:
            one.wait_send()


def on_device(vectors, links, dirs, moms):
    block = jnp.transpose(vectors, (1, 0, 2, 3)).reshape(3, 128, 1024)
    link = links.reshape(3, 18, 512)
    dma = pltpu.SemaphoreType.DMA
    vmem = pl.BlockSpec(memory_space=pltpu.VMEM)
    smem = pl.BlockSpec(memory_space=pltpu.SMEM)
    return pl.pallas_call(
        kernel,
        out_shape=jax.ShapeDtypeStruct((6, 2, 2, 8, 1024), F32),
        in_specs=[vmem, vmem, smem, smem],
        out_specs=vmem,
        scratch_shapes=[
            pltpu.VMEM((2, 8, 3, 128, 1024), BF16),
            pltpu.VMEM((6, 768, 1024), BF16),
            pltpu.VMEM((4, 12, 64, 256), F32),
            pltpu.VMEM((4, 12, 64, 256), F32),
            pltpu.VMEM((6, 64, 6 * PLANE), F32),
            pltpu.VMEM((4, 6, 64, 1024), F32),
            pltpu.VMEM((3, 18, 5 * PLANE), F32),
            pltpu.VMEM((2, 18, 1024), F32),
            pltpu.VMEM((3, 18, 512), F32),
            pltpu.VMEM((2, 18, PLANE), F32),
            pltpu.VMEM((16, 1024), F32),
            pltpu.VMEM((16, 1024), F32),
            pltpu.VMEM((2, 6, 64, PLANE), BF16),
            pltpu.VMEM((2, 6, 64, PLANE), BF16),
            pltpu.VMEM((4, 2, 12, 16, 256), BF16),
            pltpu.VMEM((4, 2, 12, 16, 256), BF16),
            pltpu.VMEM((4, 2, 24, 16, 256), BF16),
            pltpu.VMEM((4, 2, 24, 16, 256), BF16),
            pltpu.VMEM((4, 24, 16, 256), F32),
            pltpu.VMEM((4, 24, 8, 256), F32),
            pltpu.VMEM((6, 2, 2, 8, 256), F32),
            dma((4, 3)), dma((2, 3)), dma((2, 3)), dma((3,)), dma((8, 3)), dma((8, 3, 2)), dma((8, 3)),
            dma, dma, dma((2,)), dma((2,)), dma((2,)), dma((2,)),
            dma((4, 2)), dma((4, 2)), dma((4, 2)), dma((4, 2)), dma((4,)), dma((4,)),
        ],
        compiler_params=pltpu.CompilerParams(
            collective_id=0, has_side_effects=True, vmem_limit_bytes=60 * 2**20
        ),
        name="elementals",
    )(block, link, dirs, moms)


def solution(mesh):
    placed = (P("vec", None, None, "gz"), P(None, None, None, None, "gz"), P(), P())
    return jax.shard_map(
        on_device,
        mesh=mesh,
        in_specs=placed,
        out_specs=P(None, None, None, ("vec", "gz"), None),
        check_vma=False,
    )
```

time: 601 us -> 104 us (0.17)
  waiting for transfers between devices: 495 us -> 0 us
  Pallas kernels: 0 us -> 96.4 us
  matrix products: 32.9 us -> 0 us
  local copies, waits for them, and re-layouts: 32.3 us -> 6.84 us
  other arithmetic: 16.4 us -> 0 us
  between operations: 14.6 us -> 0.01 us
  starting transfers between devices: 9.11 us -> 0 us
    reduce_scatter x6 -> x0, waiting for transfers between devices: 378 us -> none  [on_device(): lax.psum_scatter(product, 'gz', scatter_dimension=2, tiled=True)]
    all_gather x1 -> x0, waiting for transfers between devices: 111 us -> none  [on_device(): gathered = lax.all_gather(vectors, 'vec', axis=0, tiled=True)]
    pallas_call x0 -> x1, Pallas kernels: none -> 96.4 us  [on_device(): pl.pallas_call(kernel, out_shape=jax.ShapeDtypeStruct((6, 2, 2, 8, 1024),...]
    dot_general x7 -> x0, matrix products: 32.9 us -> none  [the longest x6 31.9 us: on_device(): jnp.einsum('qpicrs,jcrs->pqij', left, gathered, preferred_element_type=jn...]
    unnamed x111 -> x1, local copies, waits for them, and re-layouts: 18.3 us -> 2.09 us
    ppermute x3 -> x0, starting transfers between devices: 8.46 us -> none  [the longest x1 4.36 us: on_device(): above = lax.ppermute(vectors[..., :plane], 'gz', down)]
    slice x25 -> x0, local copies, waits for them, and re-layouts: 7.65 us -> none  [the longest x1 2 us: on_device(): below = lax.ppermute(vectors[..., sites - plane:], 'gz', up)]
    ppermute x3 -> x0, waiting for transfers between devices: 6.11 us -> none  [the longest x1 6.11 us: on_device(): above = lax.ppermute(vectors[..., :plane], 'gz', down)]
  transfers between devices with their start and end apart: 10 -> 0, of which waited for: 8 -> 0; matrix products, arithmetic and copies ran while one was open for 11% -> 0% of each run, Pallas kernels for 0% -> 0%
where the time goes in v2:
time: 104 us; the launch traced here: 103 us
  Pallas kernels  96.4 us (93%)
  local copies, waits for them, and re-layouts  6.84 us (7%)
    pallas_call x1, Pallas kernels, on_device(): pl.pallas_call(kernel, out_shape=jax.ShapeDtypeStruct((6, 2, 2, 8, 1024),...  96.4 us
    unnamed x1, local copies, waits for them, and re-layouts  2.09 us

profile of v2, /device:TPU:0, one launch (start us, length us, event | category | flops | bytes accessed | tf_op | source)
XLA Modules:
  0.0 103.3 jit_solution(15639285826171135359)
XLA Ops:
  0.0 1.6 %reshape.7.u_ref = f32[3,18,512]{2,1,0:T(8,128)} reshape(f32[3,3,3,2,512]{4,3,2,1,0:T(2,128)} %param.5) | data formatting | bytes 221184 | tf_op jit(solution)/shard_map/reshape | solution.py:432
  1.6 1.7 %copy.5 = bf16[3,128,2,512]{3,2,1,0:T(2,128)(2,1)S(1)} copy(bf16[3,128,2,512]{3,2,0,1:T(2,128)(2,1)} %bitcast.1) | data formatting | bytes 1572864 | tf_op jit(solution)/shard_map/transpose | solution.py:431
  3.3 1.4 %reshape.6.v_ref = bf16[3,128,1024]{2,1,0:T(8,128)(2,1)} reshape(bf16[3,128,2,512]{3,2,1,0:T(2,128)(2,1)S(1)} %copy.5) | data formatting | bytes 1572864 | tf_op jit(solution)/shard_map/reshape | solution.py:431
  4.8 96.4 %elementals.1 = f32[6,2,2,8,1024]{4,3,2,1,0:T(8,128)} custom-call(bf16[3,128,1024]{2,1,0:T(8,128)(2,1)} %reshape.6.v_ref, f32[3,18,512]{2,1,0:T(8,128)} %reshape.7.u_ref, s32[6]{0:T(128)} %dirs_ref.1, s32[2,3]{1,0:T(2,128)} %moms_ref.1), custom_call_target="tpu_custom_call" | custom-call | tf_op jit(solution)/shard_map/elementals/pallas_call | solution.py:436
  101.2 2.1 %copy.7 = f32[6,2,2,8,1024]{4,3,2,1,0:T(8,128)} copy(f32[6,2,2,8,1024]{4,3,2,1,0:T(8,128)} %elementals.1) | data formatting | bytes 1572864

commit v3 on v2

--- a/solution.py
+++ b/solution.py
@@ -40,10 +40,10 @@
 def kernel(
     v_ref, u_ref, dirs_ref, moms_ref, o_ref,
     V, A, RE, IM, XF, XS, LK, LS, LKR, LHR, PC, PS, HS, HB,
-    S1, R1, S2, R2, T, R4, FS,
-    ss_own, ss_f01, ss_half, ss_z, ss_core, rs_ag, rs_core,
+    S1, R1, S2, R2, T, R4, FS, DS, DR,
+    ss_own, ss_f01, ss_half, ss_third, ss_cross, ss_core, rs_ag, rs_core,
     ss_link, rs_link, ss_halo, rs_halo, ss_lh, rs_lh,
-    ss_1, rs_1, ss_2, rs_2, ss_4, rs_4,
+    ss_1, rs_1, ss_2, rs_2, ss_4, rs_4, ss_d, rs_d,
 ):
     v = lax.axis_index("vec")
     g = lax.axis_index("gz")
@@ -62,11 +62,13 @@
     dev_xp = (v, (((x + 1) % 4) * 2 + zh) * 2 + core)
     dev_xm = (v, (((x + 3) % 4) * 2 + zh) * 2 + core)
     dev_zh = (v, (x * 2 + (1 - zh)) * 2 + core)
+    turn_of = [(chip + o) % 8 for o in range(8)]
     up = (chip + 1) % 8
     down = (chip + 7) % 8
     barrier = pltpu.get_barrier_semaphore()
-    everyone = [dev_core, dev_yp, dev_ym, dev_z, dev_xp, dev_xm, dev_zh]
-    everyone += [(v, up * 2), (v, up * 2 + 1), (v, down * 2), (v, down * 2 + 1)]
+    everyone = [dev_core, dev_yp, dev_ym, dev_z]
+    everyone += [(v, turn_of[o] * 2 + core) for o in range(1, 8)]
+    everyone += [(v, up * 2 + other), (v, down * 2 + other)]
     for dev in everyone:
         pl.semaphore_signal(barrier, inc=1, device_id=dev, device_id_type=MESH)
     pl.semaphore_wait(barrier, len(everyone))
@@ -81,8 +83,10 @@
             copy(v_ref.at[c], V.at[core, 0, c], ss_own.at[0, c], rs_core.at[0, c], dev_core),
             copy(v_ref.at[c], V.at[core, 3, c], ss_own.at[1, c], rs_ag.at[3, c, 0], dev_yp),
             copy(v_ref.at[c], V.at[core, 2, c], ss_own.at[2, c], rs_ag.at[2, c, 0], dev_ym),
-            copy(v_ref.at[c], V.at[core, 1, c], ss_own.at[3, c], rs_ag.at[1, c, 0], dev_z),
         ]
+
+    def own_z(c):
+        return copy(v_ref.at[c], V.at[core, 1, c], ss_own.at[3, c], rs_ag.at[1, c, 0], dev_z)
 
     def core_copy(slot, c):
         block = V.at[core, slot, c]
@@ -94,7 +98,7 @@
 
     def ag_wait(slot, c):
         block = V.at[core, slot, c]
-        copy(block, block, ss_z.at[c], rs_ag.at[slot, c, 0], dev_z).wait_recv()
+        copy(block, block, ss_third.at[c, 0], rs_ag.at[slot, c, 0], dev_z).wait_recv()
 
     def half_copies(c):
         low, high = pl.ds(0, 64), pl.ds(64, 64)
@@ -109,8 +113,18 @@
             copy(V.at[core, 1, c], V.at[core, 6, c], ss_f01.at[1, c], rs_ag.at[6, c, 0], dev_ym),
         ]
 
-    def z_copy(c):
-        return copy(V.at[core, 4, c], V.at[core, 5, c], ss_z.at[c], rs_ag.at[5, c, 0], dev_z)
+    def cross_copies():
+        return [
+            copy(V.at[core, 2, 2], V.at[core, 6, 2], ss_cross.at[0], rs_ag.at[6, 2, 0], dev_z),
+            copy(V.at[core, 3, 2], V.at[core, 7, 2], ss_cross.at[1], rs_ag.at[7, 2, 0], dev_z),
+        ]
+
+    def third(slot, c, part, dev):
+        rows = pl.ds((0, 48, 96)[part], (48, 48, 32)[part])
+        return copy(V.at[core, slot, c, rows], V.at[core, 5, c, rows], ss_third.at[c, part], rs_ag.at[5, c, part], dev)
+
+    def thirds(c):
+        return [third(6, c, 0, dev_ym), third(7, c, 1, dev_yp), third(4, c, 2, dev_z)]
 
     link_copy = copy(u_ref, LKR, ss_link, rs_link, dev_core)
     side = jnp.where(core == 1, up, down)
@@ -137,6 +151,8 @@
                 HS[half, c * 2 + r] = plane[:, half].reshape(64, PLANE).astype(BF16)
     for one in halo_copies():
         one.start()
+    for c in range(3):
+        own_z(c).start()
 
     for c in range(3):
         V[core, 0, c] = v_ref[c]
@@ -257,12 +273,20 @@
     left(2)
     left(5)
 
+    def arrive(slot, c):
+        ag_wait(slot, c)
+        core_copy(slot, c).start()
+
     def early(c):
-        for slot in (2, 3, 1):
-            ag_wait(slot, c)
-            core_copy(slot, c).start()
+        arrive(2, c)
+        arrive(3, c)
         for one in half_copies(c):
             one.start()
+
+    def half_arrive(c):
+        for one in half_copies(c):
+            one.wait_recv()
+        core_copy(4, c).start()
 
     early(0)
     early(1)
@@ -332,8 +356,10 @@
 
     def stage4(n):
         s4_copy(n).wait_recv()
-        total = (T[n, :, pl.ds(pl.multiple_of(zh * 8, 8), 8)] + R4[n]) * scale
-        total = total.reshape(2, 6, 2, 8, 256)
+        finish(n, T[n, :, pl.ds(pl.multiple_of(zh * 8, 8), 8)] + R4[n])
+
+    def finish(n, total):
+        total = (total * scale).reshape(2, 6, 2, 8, 256)
         for q in range(2):
             for k in range(6):
                 FS[k, :, q] = total[q, k]
@@ -348,6 +374,32 @@
             o_ref[d, :, :, :, lanes(col0, 128)] = block[..., 0:128]
             o_ref[d, :, :, :, lanes(col1, 128)] = block[..., 128:256]
 
+    def turn_rows(turn):
+        return pl.ds(pl.multiple_of(turn * 8, 8), 8)
+
+    def direct(o):
+        peer = turn_of[o]
+        return copy(DS.at[o], DR.at[8 - o], ss_d.at[o], rs_d.at[8 - o], (v, peer * 2 + core))
+
+    def direct_wait(o):
+        copy(DS.at[o], DR.at[o], ss_d.at[o], rs_d.at[o], dev_core).wait_recv()
+
+    def scatter():
+        for o in (2, 6, 1, 3, 5, 7, 4):
+            rows = turn_rows(turn_of[o])
+            DS[o, 0:96] = RE[2, :, rows].reshape(96, 256).astype(BF16)
+            DS[o, 96:192] = IM[2, :, rows].reshape(96, 256).astype(BF16)
+            direct(o).start()
+
+    def collect():
+        rows = turn_rows(chip)
+        total = [RE[2, :, rows].reshape(96, 256), IM[2, :, rows].reshape(96, 256)]
+        for o in range(1, 8):
+            direct_wait(o)
+            for q in range(2):
+                total[q] = total[q] + DR[o, q * 96 : q * 96 + 96].astype(F32)
+        finish(2, jnp.stack(total).reshape(24, 8, 256))
+
     def when_at(u, places, work):
         hit = functools.reduce(jnp.logical_or, [u == place for place in places])
         n = jnp.where(u == places[1], 1, jnp.where(u == places[2], 2, jnp.where(u == places[3], 3, 0)))
@@ -357,40 +409,70 @@
             work(n)
 
     def main(u, carry):
-        pair = jnp.where(u < 6, u // 3, jnp.where(u < 8, 2, jnp.where(u == 9, 2, 3)))
-        c = jnp.where(u < 6, u % 3, jnp.where(u < 8, u - 6, jnp.where(u == 8, 0, jnp.where(u == 9, 2, u - 9))))
-
-        @pl.when(u == 2)
+        c = u % 3
+        quarter = u // 3
+        pair = quarter + 1 - 2 * (quarter % 2)
+
+        @pl.when(u == 1)
         def _():
             early(2)
+            for one in cross_copies():
+                one.start()
+            arrive(1, 0)
+            for one in f01_copies(0):
+                one.start()
+
+        @pl.when(u == 3)
+        def _():
+            arrive(1, 1)
+            for one in f01_copies(1):
+                one.start()
+            half_arrive(0)
+
+        @pl.when(u == 4)
+        def _():
+            half_arrive(1)
+
+        @pl.when(u == 5)
+        def _():
+            half_arrive(2)
             for cc in range(3):
-                for one in f01_copies(cc):
-                    one.start()
-
-        @pl.when(jnp.logical_and(u >= 3, u < 6))
-        def _():
-            for one in half_copies(u - 3):
-                one.wait_recv()
-            z_copy(u - 3).start()
-            core_copy(4, u - 3).start()
-
-        @pl.when(jnp.logical_and(u >= 6, u < 12))
-        def _():
-            @pl.when(pair == 2)
-            def _():
-                ag_wait(5, c)
-                core_copy(5, c).start()
-
-            @pl.when(pair == 3)
-            def _():
-                for slot in (6, 7):
-                    ag_wait(slot, c)
-                    core_copy(slot, c).start()
-
-        when_at(u, (3, 6, 10, 12), stage1)
-        when_at(u, (5, 8, 12, 13), stage2)
-        when_at(u, (8, 11, 13, 14), stage3)
-        when_at(u, (11, 13, 14, 15), stage4)
+                third(4, cc, 2, dev_z).start()
+            arrive(1, 2)
+
+        @pl.when(quarter == 2)
+        def _():
+            arrive(6, c)
+            arrive(7, c)
+
+            for cc in range(3):
+                @pl.when(c == cc)
+                def _():
+                    third(6, cc, 0, dev_ym).start()
+                    third(7, cc, 1, dev_yp).start()
+
+        @pl.when(quarter == 3)
+        def _():
+            for cc in range(3):
+                @pl.when(c == cc)
+                def _():
+                    for one in thirds(cc):
+                        one.wait_recv()
+            core_copy(5, c).start()
+
+        when_at(u, (6, 3, 99, 9), stage1)
+        when_at(u, (8, 5, 99, 11), stage2)
+
+        @pl.when(u == 12)
+        def _():
+            scatter()
+
+        when_at(u, (10, 7, 99, 12), stage3)
+        when_at(u, (12, 10, 99, 13), stage4)
+
+        @pl.when(u == 13)
+        def _():
+            collect()
 
         @pl.when(u < 12)
         def _():
@@ -412,17 +494,24 @@
 
         return carry
 
-    lax.fori_loop(0, 16, main, 0)
+    lax.fori_loop(0, 14, main, 0)
 
     for c in range(3):
-        for one in own_copies(c) + half_copies(c) + f01_copies(c) + [z_copy(c)]:
+        for one in own_copies(c) + [own_z(c)] + half_copies(c) + thirds(c):
             one.wait_send()
+        if c < 2:
+            for one in f01_copies(c):
+                one.wait_send()
         for slot in range(1, 8):
             core_copy(slot, c).wait_send()
     link_copy.wait_send()
     for one in halo_copies():
         one.wait_send()
-    for n in range(4):
+    for one in cross_copies():
+        one.wait_send()
+    for o in range(1, 8):
+        direct(o).wait_send()
+    for n in (0, 1, 3):
         for one in s1_copies(n) + s2_copies(n) + [s4_copy(n)]:
             one.wait_send()
 
@@ -460,9 +549,11 @@
             pltpu.VMEM((4, 24, 16, 256), F32),
             pltpu.VMEM((4, 24, 8, 256), F32),
             pltpu.VMEM((6, 2, 2, 8, 256), F32),
-            dma((4, 3)), dma((2, 3)), dma((2, 3)), dma((3,)), dma((8, 3)), dma((8, 3, 2)), dma((8, 3)),
+            pltpu.VMEM((8, 192, 256), BF16),
+            pltpu.VMEM((8, 192, 256), BF16),
+            dma((4, 3)), dma((2, 3)), dma((2, 3)), dma((3, 3)), dma((2,)), dma((8, 3)), dma((8, 3, 3)), dma((8, 3)),
             dma, dma, dma((2,)), dma((2,)), dma((2,)), dma((2,)),
-            dma((4, 2)), dma((4, 2)), dma((4, 2)), dma((4, 2)), dma((4,)), dma((4,)),
+            dma((4, 2)), dma((4, 2)), dma((4, 2)), dma((4, 2)), dma((4,)), dma((4,)), dma((8,)), dma((8,)),
         ],
         compiler_params=pltpu.CompilerParams(
             collective_id=0, has_side_effects=True, vmem_limit_bytes=60 * 2**20

time: 104 us -> 88.7 us (0.85)
  Pallas kernels: 96.4 us -> 81.6 us
    pallas_call x1, Pallas kernels: 96.4 us -> 81.6 us  [on_device(): pl.pallas_call(kernel, out_shape=jax.ShapeDtypeStruct((6, 2, 2, 8, 1024),...]
where the time goes in v3:
time: 88.7 us; the launch traced here: 88.4 us
  Pallas kernels  81.6 us (92%)
  local copies, waits for them, and re-layouts  6.84 us (8%)
    pallas_call x1, Pallas kernels, on_device(): pl.pallas_call(kernel, out_shape=jax.ShapeDtypeStruct((6, 2, 2, 8, 1024),...  81.6 us
    unnamed x1, local copies, waits for them, and re-layouts  2.09 us

profile of v3, /device:TPU:0, one launch (start us, length us, event | category | flops | bytes accessed | tf_op | source)
XLA Modules:
  0.0 88.4 jit_solution(847859637546845227)
XLA Ops:
  0.0 1.6 %reshape.7.u_ref = f32[3,18,512]{2,1,0:T(8,128)} reshape(f32[3,3,3,2,512]{4,3,2,1,0:T(2,128)} %param.5) | data formatting | bytes 221184 | tf_op jit(solution)/shard_map/reshape | solution.py:521
  1.6 1.7 %copy.5 = bf16[3,128,2,512]{3,2,1,0:T(2,128)(2,1)S(1)} copy(bf16[3,128,2,512]{3,2,0,1:T(2,128)(2,1)} %bitcast.1) | data formatting | bytes 1572864 | tf_op jit(solution)/shard_map/transpose | solution.py:520
  3.3 1.4 %reshape.6.v_ref = bf16[3,128,1024]{2,1,0:T(8,128)(2,1)} reshape(bf16[3,128,2,512]{3,2,1,0:T(2,128)(2,1)S(1)} %copy.5) | data formatting | bytes 1572864 | tf_op jit(solution)/shard_map/reshape | solution.py:520
  4.8 81.6 %elementals.1 = f32[6,2,2,8,1024]{4,3,2,1,0:T(8,128)} custom-call(bf16[3,128,1024]{2,1,0:T(8,128)(2,1)} %reshape.6.v_ref, f32[3,18,512]{2,1,0:T(8,128)} %reshape.7.u_ref, s32[6]{0:T(128)} %dirs_ref.1, s32[2,3]{1,0:T(2,128)} %moms_ref.1), custom_call_target="tpu_custom_call" | custom-call | tf_op jit(solution)/shard_map/elementals/pallas_call | solution.py:525
  86.3 2.1 %copy.7 = f32[6,2,2,8,1024]{4,3,2,1,0:T(8,128)} copy(f32[6,2,2,8,1024]{4,3,2,1,0:T(8,128)} %elementals.1) | data formatting | bytes 1572864

commit v4 on v3

--- a/solution.py
+++ b/solution.py
@@ -21,29 +21,33 @@
     return pl.ds(pl.multiple_of(start, multiple), size)
 
 
+def roll(value, by):
+    return pltpu.roll(value, by, value.ndim - 1)
+
+
 def shifted(a, b, lane, kind):
     if kind == 0:
         first = lane % LX == 0
-        return [jnp.where(first, pltpu.roll(v, 97, 1), pltpu.roll(v, 1, 1)) for v in (a, b)]
+        return [jnp.where(first, roll(v, 97), roll(v, 1)) for v in (a, b)]
     if kind == 2:
         last = lane % LX == LX - 1
-        return [jnp.where(last, pltpu.roll(v, 31, 1), pltpu.roll(v, 127, 1)) for v in (a, b)]
+        return [jnp.where(last, roll(v, 31), roll(v, 127)) for v in (a, b)]
     if kind == 1:
         first = lane < LX
-        ra, rb = pltpu.roll(a, 32, 1), pltpu.roll(b, 32, 1)
+        ra, rb = roll(a, 32), roll(b, 32)
         return [jnp.where(first, rb, ra), jnp.where(first, ra, rb)]
     last = lane >= 96
-    ra, rb = pltpu.roll(a, 96, 1), pltpu.roll(b, 96, 1)
+    ra, rb = roll(a, 96), roll(b, 96)
     return [jnp.where(last, rb, ra), jnp.where(last, ra, rb)]
 
 
 def kernel(
     v_ref, u_ref, dirs_ref, moms_ref, o_ref,
     V, A, RE, IM, XF, XS, LK, LS, LKR, LHR, PC, PS, HS, HB,
-    S1, R1, S2, R2, T, R4, FS, DS, DR,
+    S1, R1, S4, R4, T, FS, DS, DR,
     ss_own, ss_f01, ss_half, ss_third, ss_cross, ss_core, rs_ag, rs_core,
     ss_link, rs_link, ss_halo, rs_halo, ss_lh, rs_lh,
-    ss_1, rs_1, ss_2, rs_2, ss_4, rs_4, ss_d, rs_d,
+    ss_1, rs_1, ss_4, rs_4, ss_d, rs_d,
 ):
     v = lax.axis_index("vec")
     g = lax.axis_index("gz")
@@ -103,28 +107,28 @@
     def half_copies(c):
         low, high = pl.ds(0, 64), pl.ds(64, 64)
         return [
-            copy(V.at[core, 2, c, low], V.at[core, 4, c, low], ss_half.at[0, c], rs_ag.at[4, c, 0], dev_ym),
-            copy(V.at[core, 3, c, high], V.at[core, 4, c, high], ss_half.at[1, c], rs_ag.at[4, c, 1], dev_yp),
+            copy(V.at[core, 2, c, :, low], V.at[core, 4, c, :, low], ss_half.at[0, c], rs_ag.at[4, c, 0], dev_ym),
+            copy(V.at[core, 3, c, :, high], V.at[core, 4, c, :, high], ss_half.at[1, c], rs_ag.at[4, c, 1], dev_yp),
         ]
 
     def f01_copies(c):
         return [
             copy(V.at[core, 1, c], V.at[core, 7, c], ss_f01.at[0, c], rs_ag.at[7, c, 0], dev_yp),
-            copy(V.at[core, 1, c], V.at[core, 6, c], ss_f01.at[1, c], rs_ag.at[6, c, 0], dev_ym),
+            copy(V.at[core, 1, c], V.at[core, 5, c], ss_f01.at[1, c], rs_ag.at[5, c, 0], dev_ym),
         ]
 
     def cross_copies():
         return [
-            copy(V.at[core, 2, 2], V.at[core, 6, 2], ss_cross.at[0], rs_ag.at[6, 2, 0], dev_z),
+            copy(V.at[core, 2, 2], V.at[core, 5, 2], ss_cross.at[0], rs_ag.at[5, 2, 0], dev_z),
             copy(V.at[core, 3, 2], V.at[core, 7, 2], ss_cross.at[1], rs_ag.at[7, 2, 0], dev_z),
         ]
 
     def third(slot, c, part, dev):
         rows = pl.ds((0, 48, 96)[part], (48, 48, 32)[part])
-        return copy(V.at[core, slot, c, rows], V.at[core, 5, c, rows], ss_third.at[c, part], rs_ag.at[5, c, part], dev)
+        return copy(V.at[core, slot, c, :, rows], V.at[core, 6, c, :, rows], ss_third.at[c, part], rs_ag.at[6, c, part], dev)
 
     def thirds(c):
-        return [third(6, c, 0, dev_ym), third(7, c, 1, dev_yp), third(4, c, 2, dev_z)]
+        return [third(5, c, 0, dev_ym), third(7, c, 1, dev_yp), third(4, c, 2, dev_z)]
 
     link_copy = copy(u_ref, LKR, ss_link, rs_link, dev_core)
     side = jnp.where(core == 1, up, down)
@@ -135,7 +139,7 @@
             dev = (v, side * 2 + half)
             pairs.append(copy(HS.at[half], HB.at[other], ss_halo.at[half], rs_halo.at[other], dev))
             pairs.append(
-                copy(u_ref.at[2, :, lanes(core * PLANE, PLANE)], LHR.at[other], ss_lh.at[half], rs_lh.at[other], dev)
+                copy(u_ref.at[2, :, :, lanes(core * PLANE, PLANE)], LHR.at[other], ss_lh.at[half], rs_lh.at[other], dev)
             )
         return pairs
 
@@ -146,7 +150,7 @@
 
     for c in range(3):
         for r in range(2):
-            plane = v_ref[c, :, lanes(r * 512 + core * PLANE, PLANE)].astype(F32).reshape(8, 2, 8, PLANE)
+            plane = v_ref[c, r, :, lanes(core * PLANE, PLANE)].astype(F32).reshape(8, 2, 8, PLANE)
             for half in range(2):
                 HS[half, c * 2 + r] = plane[:, half].reshape(64, PLANE).astype(BF16)
     for one in halo_copies():
@@ -161,13 +165,13 @@
         def body(i, carry):
             c, r = i // 2, i % 2
             for t in range(8):
-                rows = source(c, pl.ds(t * 16, 16), lanes(r * 512, 512)).astype(F32)
+                rows = source(c, r, pl.ds(t * 16, 16)).astype(F32)
                 XF[i, t * 8 : t * 8 + 8, lanes(PLANE + h * 512, 512)] = jnp.where(core == 0, rows[:8], rows[8:])
             return carry
 
         lax.fori_loop(0, 6, body, 0)
 
-    extract(core, lambda c, rows, cols: v_ref[c, rows, cols])
+    extract(core, lambda c, r, rows: v_ref[c, r, rows])
 
     site = lax.broadcasted_iota(jnp.int32, (16, 1024), 1)
     row = lax.broadcasted_iota(jnp.int32, (16, 1024), 0)
@@ -188,19 +192,19 @@
 
     link_copy.wait_recv()
     for mu in range(3):
-        LK[mu, :, lanes(PLANE + core * 512, 512)] = u_ref[mu]
-        LK[mu, :, lanes(PLANE + other * 512, 512)] = LKR[mu]
-    lane_u = lax.broadcasted_iota(jnp.int32, (18, 128), 1)
+        LK[mu, :, :, lanes(PLANE + core * 512, 512)] = u_ref[mu]
+        LK[mu, :, :, lanes(PLANE + other * 512, 512)] = LKR[mu]
+    lane_u = lax.broadcasted_iota(jnp.int32, (9, 2, 128), 2)
     for mu in range(2):
         for plane in range(4):
             start = PLANE * (plane + 1)
-            pair = shifted(LK[mu, :, start : start + 128], LK[mu, :, start + 128 : start + 256], lane_u, mu)
-            LS[mu, :, plane * PLANE : plane * PLANE + 128] = pair[0]
-            LS[mu, :, plane * PLANE + 128 : plane * PLANE + 256] = pair[1]
+            pair = shifted(LK[mu, :, :, start : start + 128], LK[mu, :, :, start + 128 : start + 256], lane_u, mu)
+            LS[mu, :, :, plane * PLANE : plane * PLANE + 128] = pair[0]
+            LS[mu, :, :, plane * PLANE + 128 : plane * PLANE + 256] = pair[1]
 
     for c in range(3):
         core_wait(0, c)
-    extract(other, lambda c, rows, cols: V[other, 0, c, rows, cols])
+    extract(other, lambda c, r, rows: V[other, 0, c, r, rows])
 
     lane_x = lax.broadcasted_iota(jnp.int32, (64, 128), 1)
 
@@ -223,10 +227,10 @@
             here = lanes(lb * 128, 128)
             h, spot = lb // 4, (lb % 4) * 128
             if k < 2:
-                link = [[[LS[mu, pl.ds((a * 3 + b) * 2 + r, 1), here] for r in range(2)] for b in range(3)] for a in range(3)]
+                link = [[[LS[mu, a * 3 + b, pl.ds(r, 1), here] for r in range(2)] for b in range(3)] for a in range(3)]
             else:
                 there = lanes(lb * 128 + (0 if k == 2 else PLANE), 128)
-                link = [[[LK[mu, pl.ds((a * 3 + b) * 2 + r, 1), there] for r in range(2)] for b in range(3)] for a in range(3)]
+                link = [[[LK[mu, a * 3 + b, pl.ds(r, 1), there] for r in range(2)] for b in range(3)] for a in range(3)]
             cs = [PC[pl.ds(k * 2 + p, 1), here] for p in range(2)]
             sn = [PS[pl.ds(k * 2 + p, 1), here] for p in range(2)]
             for ib in range(4):
@@ -269,7 +273,7 @@
     for comp in range(6):
         XF[comp, :, 0:PLANE] = HB[0, comp].astype(F32)
         XF[comp, :, 5 * PLANE : 6 * PLANE] = HB[1, comp].astype(F32)
-    LK[2, :, 0:PLANE] = LHR[0]
+    LK[2, :, :, 0:PLANE] = LHR[0]
     left(2)
     left(5)
 
@@ -293,10 +297,11 @@
 
     def product(pair, c, h):
         a = A[h * 3 + c]
-        w = V[h, pl.ds(pair * 2, 2), c].reshape(256, 1024)
-        real = lax.dot_general(a, w, NT, preferred_element_type=F32)
-        imag = lax.dot_general(a[:, :512], w[:, 512:], NT, preferred_element_type=F32)
-        imag = imag - lax.dot_general(a[:, 512:], w[:, :512], NT, preferred_element_type=F32)
+        w = V[h, pl.ds(pair * 2, 2), c]
+        wr, wi = w[:, 0].reshape(256, 512), w[:, 1].reshape(256, 512)
+        real = lax.dot_general(a, jnp.concatenate((wr, wi), axis=1), NT, preferred_element_type=F32)
+        imag = lax.dot_general(a[:, :512], wi, NT, preferred_element_type=F32)
+        imag = imag - lax.dot_general(a[:, 512:], wr, NT, preferred_element_type=F32)
         real = real.reshape(12, 64, 256)
         imag = imag.reshape(12, 64, 256)
         fresh = jnp.logical_and(c == 0, h == core)
@@ -314,57 +319,47 @@
     def rows_of(xx):
         return pl.ds(pl.multiple_of((xx % 4) * 16, 16), 16)
 
-    def s1_copies(n):
-        return [
-            copy(S1.at[n, 0], R1.at[n, 0], ss_1.at[n, 0], rs_1.at[n, 0], dev_xp),
-            copy(S1.at[n, 1], R1.at[n, 1], ss_1.at[n, 1], rs_1.at[n, 1], dev_xm),
-        ]
-
-    def s2_copies(n):
-        return [
-            copy(S2.at[n, 0], R2.at[n, 0], ss_2.at[n, 0], rs_2.at[n, 0], dev_xp),
-            copy(S2.at[n, 1], R2.at[n, 1], ss_2.at[n, 1], rs_2.at[n, 1], dev_xm),
-        ]
-
-    def s4_copy(n):
-        return copy(T.at[n, :, pl.ds(pl.multiple_of((1 - zh) * 8, 8), 8)], R4.at[n], ss_4.at[n], rs_4.at[n], dev_zh)
+    def x_copy(n, o):
+        dev = (v, (((x + o) % 4) * 2 + zh) * 2 + core)
+        return copy(S1.at[n, o], R1.at[n, 4 - o], ss_1.at[n, o], rs_1.at[n, 4 - o], dev)
+
+    def x_wait(n, o):
+        copy(S1.at[n, o], R1.at[n, o], ss_1.at[n, o], rs_1.at[n, o], dev_core).wait_recv()
+
+    def z_copy(n):
+        return copy(S4.at[n], R4.at[n], ss_4.at[n], rs_4.at[n], dev_zh)
 
     def stage1(n):
-        S1[n, 0] = RE[n, :, rows_of(x + 2)].astype(BF16)
-        S1[n, 1] = IM[n, :, rows_of(x + 2)].astype(BF16)
-        for one in s1_copies(n):
-            one.start()
+        for o in (2, 1, 3):
+            S1[n, o, 0:12] = RE[n, :, rows_of(x + o)].astype(BF16)
+            S1[n, o, 12:24] = IM[n, :, rows_of(x + o)].astype(BF16)
+            x_copy(n, o).start()
 
     def stage2(n):
-        for one in s1_copies(n):
-            one.wait_recv()
-        S2[n, 0, 0:12] = (RE[n, :, rows_of(x + 1)] + R1[n, 0].astype(F32)).astype(BF16)
-        S2[n, 0, 12:24] = IM[n, :, rows_of(x + 1)].astype(BF16)
-        S2[n, 1, 0:12] = RE[n, :, rows_of(x + 3)].astype(BF16)
-        S2[n, 1, 12:24] = (IM[n, :, rows_of(x + 3)] + R1[n, 1].astype(F32)).astype(BF16)
-        for one in s2_copies(n):
-            one.start()
+        for o in (1, 2, 3):
+            x_wait(n, o)
+        for q, part in ((0, RE), (1, IM)):
+            total = part[n, :, rows_of(x)]
+            for o in (1, 2, 3):
+                total = total + R1[n, o, q * 12 : q * 12 + 12].astype(F32)
+            low, high = total[:, 0:8], total[:, 8:16]
+            T[n, q * 12 : q * 12 + 12] = jnp.where(zh == 0, low, high)
+            S4[n, q * 96 : q * 96 + 96] = jnp.where(zh == 0, high, low).reshape(96, 256).astype(BF16)
+        z_copy(n).start()
+
+    scale = 1.0 / math.sqrt(3.0 * 8192)
 
     def stage3(n):
-        for one in s2_copies(n):
-            one.wait_recv()
-        T[n, 0:12] = RE[n, :, rows_of(x)] + (R2[n, 0, 0:12].astype(F32) + R2[n, 1, 0:12].astype(F32))
-        T[n, 12:24] = IM[n, :, rows_of(x)] + (R2[n, 0, 12:24].astype(F32) + R2[n, 1, 12:24].astype(F32))
-        s4_copy(n).start()
-
-    scale = 1.0 / math.sqrt(3.0 * 8192)
-
-    def stage4(n):
-        s4_copy(n).wait_recv()
-        finish(n, T[n, :, pl.ds(pl.multiple_of(zh * 8, 8), 8)] + R4[n])
+        z_copy(n).wait_recv()
+        finish(n, T[n] + R4[n].astype(F32).reshape(24, 8, 256))
 
     def finish(n, total):
         total = (total * scale).reshape(2, 6, 2, 8, 256)
         for q in range(2):
             for k in range(6):
                 FS[k, :, q] = total[q, k]
-        dy0 = jnp.where(n == 0, 0, jnp.where(n == 2, 2, 1))
-        dy1 = jnp.where(n == 0, 0, jnp.where(n == 2, 2, 3))
+        dy0 = jnp.where(n == 0, 0, jnp.where(n == 1, 1, 2))
+        dy1 = jnp.where(n == 0, 0, jnp.where(n == 2, 1, 3))
         z0 = jnp.where(n == 3, 1 - zl, zl)
         z1 = jnp.where(n == 1, zl, 1 - zl)
         col0 = at(y + dy0, z0) * 128
@@ -387,31 +382,31 @@
     def scatter():
         for o in (2, 6, 1, 3, 5, 7, 4):
             rows = turn_rows(turn_of[o])
-            DS[o, 0:96] = RE[2, :, rows].reshape(96, 256).astype(BF16)
-            DS[o, 96:192] = IM[2, :, rows].reshape(96, 256).astype(BF16)
+            DS[o, 0:96] = RE[3, :, rows].reshape(96, 256).astype(BF16)
+            DS[o, 96:192] = IM[3, :, rows].reshape(96, 256).astype(BF16)
             direct(o).start()
 
     def collect():
         rows = turn_rows(chip)
-        total = [RE[2, :, rows].reshape(96, 256), IM[2, :, rows].reshape(96, 256)]
+        total = [RE[3, :, rows].reshape(96, 256), IM[3, :, rows].reshape(96, 256)]
         for o in range(1, 8):
             direct_wait(o)
             for q in range(2):
                 total[q] = total[q] + DR[o, q * 96 : q * 96 + 96].astype(F32)
-        finish(2, jnp.stack(total).reshape(24, 8, 256))
+        finish(3, jnp.stack(total).reshape(24, 8, 256))
 
     def when_at(u, places, work):
         hit = functools.reduce(jnp.logical_or, [u == place for place in places])
-        n = jnp.where(u == places[1], 1, jnp.where(u == places[2], 2, jnp.where(u == places[3], 3, 0)))
+        n = jnp.where(u == places[1], 1, jnp.where(u == places[2], 2, 0))
 
         @pl.when(hit)
         def _():
             work(n)
 
     def main(u, carry):
-        c = u % 3
         quarter = u // 3
-        pair = quarter + 1 - 2 * (quarter % 2)
+        c = jnp.where(quarter < 2, u % 3, (3 - u % 3) % 3)
+        pair = jnp.where(quarter < 2, 1 - quarter, quarter)
 
         @pl.when(u == 1)
         def _():
@@ -436,20 +431,30 @@
         @pl.when(u == 5)
         def _():
             half_arrive(2)
-            for cc in range(3):
+            for cc in (0, 2, 1):
                 third(4, cc, 2, dev_z).start()
             arrive(1, 2)
 
-        @pl.when(quarter == 2)
-        def _():
-            arrive(6, c)
-            arrive(7, c)
-
-            for cc in range(3):
-                @pl.when(c == cc)
-                def _():
-                    third(6, cc, 0, dev_ym).start()
-                    third(7, cc, 1, dev_yp).start()
+        @pl.when(u == 6)
+        def _():
+            arrive(5, 0)
+            third(5, 0, 0, dev_ym).start()
+            arrive(7, 0)
+            third(7, 0, 1, dev_yp).start()
+
+        @pl.when(u == 7)
+        def _():
+            arrive(5, 2)
+            third(5, 2, 0, dev_ym).start()
+
+        @pl.when(u == 8)
+        def _():
+            arrive(5, 1)
+            third(5, 1, 0, dev_ym).start()
+            arrive(7, 2)
+            third(7, 2, 1, dev_yp).start()
+            arrive(7, 1)
+            third(7, 1, 1, dev_yp).start()
 
         @pl.when(quarter == 3)
         def _():
@@ -458,17 +463,15 @@
                 def _():
                     for one in thirds(cc):
                         one.wait_recv()
-            core_copy(5, c).start()
-
-        when_at(u, (6, 3, 99, 9), stage1)
-        when_at(u, (8, 5, 99, 11), stage2)
+            core_copy(6, c).start()
 
         @pl.when(u == 12)
         def _():
             scatter()
 
-        when_at(u, (10, 7, 99, 12), stage3)
-        when_at(u, (12, 10, 99, 13), stage4)
+        when_at(u, (6, 3, 9), stage1)
+        when_at(u, (10, 6, 12), stage2)
+        when_at(u, (12, 9, 13), stage3)
 
         @pl.when(u == 13)
         def _():
@@ -511,14 +514,15 @@
         one.wait_send()
     for o in range(1, 8):
         direct(o).wait_send()
-    for n in (0, 1, 3):
-        for one in s1_copies(n) + s2_copies(n) + [s4_copy(n)]:
-            one.wait_send()
+    for n in range(3):
+        for o in range(1, 4):
+            x_copy(n, o).wait_send()
+        z_copy(n).wait_send()
 
 
 def on_device(vectors, links, dirs, moms):
-    block = jnp.transpose(vectors, (1, 0, 2, 3)).reshape(3, 128, 1024)
-    link = links.reshape(3, 18, 512)
+    block = jnp.transpose(vectors, (1, 2, 0, 3))
+    link = links.reshape(3, 9, 2, 512)
     dma = pltpu.SemaphoreType.DMA
     vmem = pl.BlockSpec(memory_space=pltpu.VMEM)
     smem = pl.BlockSpec(memory_space=pltpu.SMEM)
@@ -528,32 +532,31 @@
         in_specs=[vmem, vmem, smem, smem],
         out_specs=vmem,
         scratch_shapes=[
-            pltpu.VMEM((2, 8, 3, 128, 1024), BF16),
+            pltpu.VMEM((2, 8, 3, 2, 128, 512), BF16),
             pltpu.VMEM((6, 768, 1024), BF16),
             pltpu.VMEM((4, 12, 64, 256), F32),
             pltpu.VMEM((4, 12, 64, 256), F32),
             pltpu.VMEM((6, 64, 6 * PLANE), F32),
             pltpu.VMEM((4, 6, 64, 1024), F32),
-            pltpu.VMEM((3, 18, 5 * PLANE), F32),
-            pltpu.VMEM((2, 18, 1024), F32),
-            pltpu.VMEM((3, 18, 512), F32),
-            pltpu.VMEM((2, 18, PLANE), F32),
+            pltpu.VMEM((3, 9, 2, 5 * PLANE), F32),
+            pltpu.VMEM((2, 9, 2, 1024), F32),
+            pltpu.VMEM((3, 9, 2, 512), F32),
+            pltpu.VMEM((2, 9, 2, PLANE), F32),
             pltpu.VMEM((16, 1024), F32),
             pltpu.VMEM((16, 1024), F32),
             pltpu.VMEM((2, 6, 64, PLANE), BF16),
             pltpu.VMEM((2, 6, 64, PLANE), BF16),
-            pltpu.VMEM((4, 2, 12, 16, 256), BF16),
-            pltpu.VMEM((4, 2, 12, 16, 256), BF16),
-            pltpu.VMEM((4, 2, 24, 16, 256), BF16),
-            pltpu.VMEM((4, 2, 24, 16, 256), BF16),
-            pltpu.VMEM((4, 24, 16, 256), F32),
-            pltpu.VMEM((4, 24, 8, 256), F32),
+            pltpu.VMEM((3, 4, 24, 16, 256), BF16),
+            pltpu.VMEM((3, 4, 24, 16, 256), BF16),
+            pltpu.VMEM((3, 192, 256), BF16),
+            pltpu.VMEM((3, 192, 256), BF16),
+            pltpu.VMEM((3, 24, 8, 256), F32),
             pltpu.VMEM((6, 2, 2, 8, 256), F32),
             pltpu.VMEM((8, 192, 256), BF16),
             pltpu.VMEM((8, 192, 256), BF16),
             dma((4, 3)), dma((2, 3)), dma((2, 3)), dma((3, 3)), dma((2,)), dma((8, 3)), dma((8, 3, 3)), dma((8, 3)),
             dma, dma, dma((2,)), dma((2,)), dma((2,)), dma((2,)),
-            dma((4, 2)), dma((4, 2)), dma((4, 2)), dma((4, 2)), dma((4,)), dma((4,)), dma((8,)), dma((8,)),
+            dma((3, 4)), dma((3, 4)), dma((3,)), dma((3,)), dma((8,)), dma((8,)),
         ],
         compiler_params=pltpu.CompilerParams(
             collective_id=0, has_side_effects=True, vmem_limit_bytes=60 * 2**20

time: 88.7 us -> 83.1 us (0.937)
  Pallas kernels: 81.6 us -> 78.2 us
  local copies, waits for them, and re-layouts: 6.84 us -> 4.19 us
    pallas_call x1, Pallas kernels: 81.6 us -> 78.2 us  [on_device(): pl.pallas_call(kernel, out_shape=jax.ShapeDtypeStruct((6, 2, 2, 8, 1024),...]
    reshape x2 -> x0, local copies, waits for them, and re-layouts: 3.08 us -> none  [the longest x1 1.64 us: on_device(): link = links.reshape(3, 18, 512)]
    unnamed x1 -> x2, local copies, waits for them, and re-layouts: 2.09 us -> 4.19 us
    transpose x1 -> x0, local copies, waits for them, and re-layouts: 1.67 us -> none  [on_device(): block = jnp.transpose(vectors, (1, 0, 2, 3)).reshape(3, 128, 1024)]
where the time goes in v4:
time: 83.1 us; the launch traced here: 82.4 us
  Pallas kernels  78.2 us (94%)
  local copies, waits for them, and re-layouts  4.19 us (5%)
    pallas_call x1, Pallas kernels, on_device(): pl.pallas_call(kernel, out_shape=jax.ShapeDtypeStruct((6, 2, 2, 8, 1024),...  78.2 us
    unnamed x2, local copies, waits for them, and re-layouts  4.19 us

profile of v4, /device:TPU:0, one launch (start us, length us, event | category | flops | bytes accessed | tf_op | source)
XLA Modules:
  0.0 82.4 jit_solution(13253134069165209638)
XLA Ops:
  0.0 2.1 %copy.7 = bf16[128,3,2,512]{3,0,2,1:T(8,128)(2,1)} copy(bf16[128,3,2,512]{3,2,1,0:T(2,128)(2,1)} %param.4) | data formatting | bytes 1572864 | tf_op args[0]
  2.1 78.2 %elementals.1 = f32[6,2,2,8,1024]{4,3,2,1,0:T(8,128)} custom-call(bf16[3,2,128,512]{3,2,1,0:T(8,128)(2,1)} %bitcast.4, f32[3,9,2,512]{3,2,1,0:T(2,128)} %bitcast.5, s32[6]{0:T(128)} %dirs_ref.1, s32[2,3]{1,0:T(2,128)} %moms_ref.1), custom_call_target="tpu_custom_call" | custom-call | tf_op jit(solution)/shard_map/elementals/pallas_call | solution.py:529
  80.3 2.1 %copy.9 = f32[6,2,2,8,1024]{4,3,2,1,0:T(8,128)} copy(f32[6,2,2,8,1024]{4,3,2,1,0:T(8,128)} %elementals.1) | data formatting | bytes 1572864

commit v5 on v4

--- a/solution.py
+++ b/solution.py
@@ -124,7 +124,7 @@
         ]
 
     def third(slot, c, part, dev):
-        rows = pl.ds((0, 48, 96)[part], (48, 48, 32)[part])
+        rows = pl.ds((0, 64, 112)[part], (64, 48, 16)[part])
         return copy(V.at[core, slot, c, :, rows], V.at[core, 6, c, :, rows], ss_third.at[c, part], rs_ag.at[6, c, part], dev)
 
     def thirds(c):
@@ -160,6 +160,13 @@
 
     for c in range(3):
         V[core, 0, c] = v_ref[c]
+
+    def clear(i, carry):
+        RE[i] = jnp.zeros((12, 64, 256), F32)
+        IM[i] = jnp.zeros((12, 64, 256), F32)
+        return carry
+
+    lax.fori_loop(0, 4, clear, 0)
 
     def extract(h, source):
         def body(i, carry):
@@ -304,17 +311,8 @@
         imag = imag - lax.dot_general(a[:, 512:], wr, NT, preferred_element_type=F32)
         real = real.reshape(12, 64, 256)
         imag = imag.reshape(12, 64, 256)
-        fresh = jnp.logical_and(c == 0, h == core)
-
-        @pl.when(fresh)
-        def _():
-            RE[pair] = real
-            IM[pair] = imag
-
-        @pl.when(jnp.logical_not(fresh))
-        def _():
-            RE[pair] += real
-            IM[pair] += imag
+        RE[pair] += real
+        IM[pair] += imag
 
     def rows_of(xx):
         return pl.ds(pl.multiple_of((xx % 4) * 16, 16), 16)
@@ -372,32 +370,36 @@
     def turn_rows(turn):
         return pl.ds(pl.multiple_of(turn * 8, 8), 8)
 
-    def direct(o):
+    def direct(n, o):
+        m = n - 2
         peer = turn_of[o]
-        return copy(DS.at[o], DR.at[8 - o], ss_d.at[o], rs_d.at[8 - o], (v, peer * 2 + core))
-
-    def direct_wait(o):
-        copy(DS.at[o], DR.at[o], ss_d.at[o], rs_d.at[o], dev_core).wait_recv()
-
-    def scatter():
+        return copy(DS.at[m, o], DR.at[m, 8 - o], ss_d.at[m, o], rs_d.at[m, 8 - o], (v, peer * 2 + core))
+
+    def direct_wait(n, o):
+        m = n - 2
+        copy(DS.at[m, o], DR.at[m, o], ss_d.at[m, o], rs_d.at[m, o], dev_core).wait_recv()
+
+    def scatter(n):
         for o in (2, 6, 1, 3, 5, 7, 4):
             rows = turn_rows(turn_of[o])
-            DS[o, 0:96] = RE[3, :, rows].reshape(96, 256).astype(BF16)
-            DS[o, 96:192] = IM[3, :, rows].reshape(96, 256).astype(BF16)
-            direct(o).start()
-
-    def collect():
+            DS[n - 2, o, 0:96] = RE[n, :, rows].reshape(96, 256).astype(BF16)
+            DS[n - 2, o, 96:192] = IM[n, :, rows].reshape(96, 256).astype(BF16)
+            direct(n, o).start()
+
+    def collect(n):
         rows = turn_rows(chip)
-        total = [RE[3, :, rows].reshape(96, 256), IM[3, :, rows].reshape(96, 256)]
+        total = [RE[n, :, rows].reshape(96, 256), IM[n, :, rows].reshape(96, 256)]
         for o in range(1, 8):
-            direct_wait(o)
+            direct_wait(n, o)
             for q in range(2):
-                total[q] = total[q] + DR[o, q * 96 : q * 96 + 96].astype(F32)
-        finish(3, jnp.stack(total).reshape(24, 8, 256))
+                total[q] = total[q] + DR[n - 2, o, q * 96 : q * 96 + 96].astype(F32)
+        finish(n, jnp.stack(total).reshape(24, 8, 256))
 
     def when_at(u, places, work):
         hit = functools.reduce(jnp.logical_or, [u == place for place in places])
-        n = jnp.where(u == places[1], 1, jnp.where(u == places[2], 2, 0))
+        n = jnp.int32(0)
+        for i, place in enumerate(places):
+            n = jnp.where(u == place, i, n)
 
         @pl.when(hit)
         def _():
@@ -407,6 +409,9 @@
         quarter = u // 3
         c = jnp.where(quarter < 2, u % 3, (3 - u % 3) % 3)
         pair = jnp.where(quarter < 2, 1 - quarter, quarter)
+
+        when_at(u, (6, 3), stage1)
+        when_at(u, (99, 99, 9, 12), scatter)
 
         @pl.when(u == 1)
         def _():
@@ -465,17 +470,9 @@
                         one.wait_recv()
             core_copy(6, c).start()
 
-        @pl.when(u == 12)
-        def _():
-            scatter()
-
-        when_at(u, (6, 3, 9), stage1)
-        when_at(u, (10, 6, 12), stage2)
-        when_at(u, (12, 9, 13), stage3)
-
-        @pl.when(u == 13)
-        def _():
-            collect()
+        when_at(u, (10, 6), stage2)
+        when_at(u, (12, 9), stage3)
+        when_at(u, (99, 99, 12, 13), collect)
 
         @pl.when(u < 12)
         def _():
@@ -513,8 +510,9 @@
     for one in cross_copies():
         one.wait_send()
     for o in range(1, 8):
-        direct(o).wait_send()
-    for n in range(3):
+        for n in (2, 3):
+            direct(n, o).wait_send()
+    for n in range(2):
         for o in range(1, 4):
             x_copy(n, o).wait_send()
         z_copy(n).wait_send()
@@ -546,17 +544,17 @@
             pltpu.VMEM((16, 1024), F32),
             pltpu.VMEM((2, 6, 64, PLANE), BF16),
             pltpu.VMEM((2, 6, 64, PLANE), BF16),
-            pltpu.VMEM((3, 4, 24, 16, 256), BF16),
-            pltpu.VMEM((3, 4, 24, 16, 256), BF16),
-            pltpu.VMEM((3, 192, 256), BF16),
-            pltpu.VMEM((3, 192, 256), BF16),
-            pltpu.VMEM((3, 24, 8, 256), F32),
+            pltpu.VMEM((2, 4, 24, 16, 256), BF16),
+            pltpu.VMEM((2, 4, 24, 16, 256), BF16),
+            pltpu.VMEM((2, 192, 256), BF16),
+            pltpu.VMEM((2, 192, 256), BF16),
+            pltpu.VMEM((2, 24, 8, 256), F32),
             pltpu.VMEM((6, 2, 2, 8, 256), F32),
-            pltpu.VMEM((8, 192, 256), BF16),
-            pltpu.VMEM((8, 192, 256), BF16),
+            pltpu.VMEM((2, 8, 192, 256), BF16),
+            pltpu.VMEM((2, 8, 192, 256), BF16),
             dma((4, 3)), dma((2, 3)), dma((2, 3)), dma((3, 3)), dma((2,)), dma((8, 3)), dma((8, 3, 3)), dma((8, 3)),
             dma, dma, dma((2,)), dma((2,)), dma((2,)), dma((2,)),
-            dma((3, 4)), dma((3, 4)), dma((3,)), dma((3,)), dma((8,)), dma((8,)),
+            dma((2, 4)), dma((2, 4)), dma((2,)), dma((2,)), dma((2, 8)), dma((2, 8)),
         ],
         compiler_params=pltpu.CompilerParams(
             collective_id=0, has_side_effects=True, vmem_limit_bytes=60 * 2**20

time: 83.1 us -> 81.3 us (0.978)
  Pallas kernels: 78.2 us -> 76.9 us
    pallas_call x1, Pallas kernels: 78.2 us -> 76.9 us  [on_device(): pl.pallas_call(kernel, out_shape=jax.ShapeDtypeStruct((6, 2, 2, 8, 1024),...]
where the time goes in v5:
time: 81.3 us; the launch traced here: 81.1 us
  Pallas kernels  76.9 us (95%)
  local copies, waits for them, and re-layouts  4.19 us (5%)
    pallas_call x1, Pallas kernels, on_device(): pl.pallas_call(kernel, out_shape=jax.ShapeDtypeStruct((6, 2, 2, 8, 1024),...  76.9 us
    unnamed x2, local copies, waits for them, and re-layouts  4.19 us

profile of v5, /device:TPU:0, one launch (start us, length us, event | category | flops | bytes accessed | tf_op | source)
XLA Modules:
  0.0 81.1 jit_solution(7270189467407633391)
XLA Ops:
  0.0 2.1 %copy.7 = bf16[128,3,2,512]{3,0,2,1:T(8,128)(2,1)} copy(bf16[128,3,2,512]{3,2,1,0:T(2,128)(2,1)} %param.4) | data formatting | bytes 1572864 | tf_op args[0]
  2.1 76.9 %elementals.1 = f32[6,2,2,8,1024]{4,3,2,1,0:T(8,128)} custom-call(bf16[3,2,128,512]{3,2,1,0:T(8,128)(2,1)} %bitcast.4, f32[3,9,2,512]{3,2,1,0:T(2,128)} %bitcast.5, s32[6]{0:T(128)} %dirs_ref.1, s32[2,3]{1,0:T(2,128)} %moms_ref.1), custom_call_target="tpu_custom_call" | custom-call | tf_op jit(solution)/shard_map/elementals/pallas_call | solution.py:527
  79.0 2.1 %copy.9 = f32[6,2,2,8,1024]{4,3,2,1,0:T(8,128)} copy(f32[6,2,2,8,1024]{4,3,2,1,0:T(8,128)} %elementals.1) | data formatting | bytes 1572864

commit v6 on v5

--- a/solution.py
+++ b/solution.py
@@ -75,6 +75,11 @@
     everyone += [(v, up * 2 + other), (v, down * 2 + other)]
     for dev in everyone:
         pl.semaphore_signal(barrier, inc=1, device_id=dev, device_id_type=MESH)
+    for c in range(3):
+        for r in range(2):
+            plane = v_ref[c, r, :, lanes(core * PLANE, PLANE)].astype(F32).reshape(8, 2, 8, PLANE)
+            for half in range(2):
+                HS[half, c * 2 + r] = plane[:, half].reshape(64, PLANE).astype(BF16)
     pl.semaphore_wait(barrier, len(everyone))
 
     def copy(src, dst, ss, rs, dev):
@@ -148,11 +153,6 @@
             one.start()
     link_copy.start()
 
-    for c in range(3):
-        for r in range(2):
-            plane = v_ref[c, r, :, lanes(core * PLANE, PLANE)].astype(F32).reshape(8, 2, 8, PLANE)
-            for half in range(2):
-                HS[half, c * 2 + r] = plane[:, half].reshape(64, PLANE).astype(BF16)
     for one in halo_copies():
         one.start()
     for c in range(3):
@@ -270,10 +270,27 @@
 
         lax.fori_loop(0, 8, body, 0)
 
+    def arrive(slot, c):
+        ag_wait(slot, c)
+        core_copy(slot, c).start()
+
+    def early(c):
+        arrive(2, c)
+        arrive(3, c)
+        for one in half_copies(c):
+            one.start()
+
+    def half_arrive(c):
+        for one in half_copies(c):
+            one.wait_recv()
+        core_copy(4, c).start()
+
     left(0)
     left(1)
     left(3)
     left(4)
+    early(0)
+    early(1)
     for one in range(2):
         copy(HS.at[0], HB.at[one], ss_halo.at[0], rs_halo.at[one], dev_core).wait_recv()
         copy(LHR.at[one], LHR.at[one], ss_lh.at[0], rs_lh.at[one], dev_core).wait_recv()
@@ -284,31 +301,12 @@
     left(2)
     left(5)
 
-    def arrive(slot, c):
-        ag_wait(slot, c)
-        core_copy(slot, c).start()
-
-    def early(c):
-        arrive(2, c)
-        arrive(3, c)
-        for one in half_copies(c):
-            one.start()
-
-    def half_arrive(c):
-        for one in half_copies(c):
-            one.wait_recv()
-        core_copy(4, c).start()
-
-    early(0)
-    early(1)
-
     def product(pair, c, h):
         a = A[h * 3 + c]
         w = V[h, pl.ds(pair * 2, 2), c]
         wr, wi = w[:, 0].reshape(256, 512), w[:, 1].reshape(256, 512)
         real = lax.dot_general(a, jnp.concatenate((wr, wi), axis=1), NT, preferred_element_type=F32)
-        imag = lax.dot_general(a[:, :512], wi, NT, preferred_element_type=F32)
-        imag = imag - lax.dot_general(a[:, 512:], wr, NT, preferred_element_type=F32)
+        imag = lax.dot_general(a, jnp.concatenate((wi, -wr), axis=1), NT, preferred_element_type=F32)
         real = real.reshape(12, 64, 256)
         imag = imag.reshape(12, 64, 256)
         RE[pair] += real

time: 81.3 us -> 81.3 us (level)
  no operation moved by 1% of the time
where the time goes in v6:
time: 81.3 us; the launch traced here: 81.1 us
  Pallas kernels  76.9 us (95%)
  local copies, waits for them, and re-layouts  4.19 us (5%)
    pallas_call x1, Pallas kernels, on_device(): pl.pallas_call(kernel, out_shape=jax.ShapeDtypeStruct((6, 2, 2, 8, 1024),...  76.9 us
    unnamed x2, local copies, waits for them, and re-layouts  4.19 us

profile of v6, /device:TPU:0, one launch (start us, length us, event | category | flops | bytes accessed | tf_op | source)
XLA Modules:
  0.0 81.1 jit_solution(1245937047452236683)
XLA Ops:
  0.0 2.1 %copy.7 = bf16[128,3,2,512]{3,0,2,1:T(8,128)(2,1)} copy(bf16[128,3,2,512]{3,2,1,0:T(2,128)(2,1)} %param.4) | data formatting | bytes 1572864 | tf_op args[0]
  2.1 76.9 %elementals.1 = f32[6,2,2,8,1024]{4,3,2,1,0:T(8,128)} custom-call(bf16[3,2,128,512]{3,2,1,0:T(8,128)(2,1)} %bitcast.4, f32[3,9,2,512]{3,2,1,0:T(2,128)} %bitcast.5, s32[6]{0:T(128)} %dirs_ref.1, s32[2,3]{1,0:T(2,128)} %moms_ref.1), custom_call_target="tpu_custom_call" | custom-call | tf_op jit(solution)/shard_map/elementals/pallas_call | solution.py:525
  79.0 2.1 %copy.9 = f32[6,2,2,8,1024]{4,3,2,1,0:T(8,128)} copy(f32[6,2,2,8,1024]{4,3,2,1,0:T(8,128)} %elementals.1) | data formatting | bytes 1572864
